TPU v7x, 256 devices: a whole 4x4x8 slice. The times are simulated.
256 devices in a mesh: row: 16 (over z, y_hi), col: 16 (over y_lo, x, core).
Axes of the slice: x: 4, y: 4 (y_hi: 2, y_lo: 2; y = y_hi * 2 + y_lo), z: 8, core: 2. Of those that a mesh axis runs over, the one named last changes fastest.
Arguments:
- anc_inverse: float32 [20480, 20480], P('row', 'col'), may hold values from -6 to 6
- l_store: float32 [16, 20480, 256], P('col', 'row'), may hold values from -0.0546875 to 0.0546875
- diag_inv: float32 [16, 256, 256], P('col'), may hold values from -6 to 6
- block_lists: int32 [4, 96], replicated, may hold values from 0 to 159, as said below
- block_counts: int32 [4], replicated, may hold values from 48 to 96, as said below
- sibling_columns: int32 [4], replicated, may hold values from 0 to 15, as said below
Outputs:
- upper_out: float32 [4, 256, 20480], P(None, 'row', 'col')
- lower_out: float32 [16, 20480, 256], P('col', 'row')
- diag_out: float32 [16, 256, 256], P('col')
Inputs may be any that keep to these rules, and one draw needn't show every extreme that they name: `block_lists`: in each sibling's row the entries are distinct block indices; entries at positions from block_counts onward are ignored. `block_counts`: some sibling uses all 96 entries. `sibling_columns`: distinct columns for distinct siblings.
All inputs are finite; a program needn't handle non-finite values.
Results may differ from a plain program's by a relative error of at most 0.00011.
Values sent between devices are 32-bit elements; how exact they have to be, the bound alone decides.
No kernel may reach another device: no remote copies, remote signals or barrier semaphores. Data moves between devices by JAX's collectives and lax.ppermute only.
A program may use at most 64 MiB of HBM per device.

v0:
```python
import jax
import jax.numpy as jnp
from jax import lax
from jax.sharding import Mesh
from jax.sharding import PartitionSpec as P

BLK = 128
ROW = ("row_0", "row_1")


def padded_to(lines, length):
    spare = -len(lines) % length
    return jnp.pad(lines, [(0, spare)] + [(0, 0)] * (lines.ndim - 1))


def total_of(x, axis):
    lines = x.reshape(-1, *x.shape[1:][-1:])
    padded = padded_to(lines, lax.axis_size(axis))
    own = lax.psum_scatter(padded, axis, scatter_dimension=0, tiled=True)
    whole = lax.all_gather(own, axis, axis=0, tiled=True)
    return whole[: len(lines)].reshape(x.shape)


def summed_rows(x, axes, dim):
    if not axes:
        return x
    nearer = lax.psum_scatter(x, axes[0], scatter_dimension=dim, tiled=True)
    return summed_rows(nearer, axes[1:], dim)


def joined_along(parts, dim):
    shape = list(parts.shape[1:])
    shape[dim] *= parts.shape[0]
    return jnp.moveaxis(parts, 0, dim).reshape(shape)


def from_everyone(x, axis):
    length = lax.axis_size(axis)
    return lax.all_to_all(jnp.broadcast_to(x[None], (length, *x.shape)), axis, 0, 0, tiled=True)


def collect(x, axis, dim):
    return joined_along(from_everyone(x, axis), dim)


def cut_along(x, dim, length):
    shape = x.shape
    parts = x.reshape(*shape[:dim], length, shape[dim] // length, *shape[dim + 1 :])
    return jnp.moveaxis(parts, dim, 0)


def sum_at_owner(x, axis, dim):
    length = lax.axis_size(axis)
    parts = lax.all_to_all(cut_along(x, dim, length), axis, 0, 0, tiled=True)
    return jnp.sum(parts, axis=0)


def nested_sum(x, axes):
    lines = x.reshape(-1, x.shape[-1])
    padded = padded_to(lines, lax.axis_size(axes))
    whole = collect(sum_at_owner(padded, axes, 0), axes, 0)
    return lax.slice_in_dim(whole, 0, len(lines)).reshape(x.shape)


def listed_blocks(block_lists, block_counts, first_block, block_total):
    block_ids = first_block + jnp.arange(block_total, dtype=jnp.int32)
    valid_entry = jnp.arange(block_lists.shape[1], dtype=jnp.int32)[None, :] < block_counts[:, None]
    entry_hits = (block_lists[:, :, None] == block_ids[None, None, :]) & valid_entry[:, :, None]
    return jnp.repeat(jnp.any(entry_hits, axis=1).astype(jnp.float32), BLK, axis=1)


def per_device(anc_inverse, l_store, diag_inv, block_lists, block_counts, sibling_columns):
    row_cells = anc_inverse.shape[0]
    col_cells = anc_inverse.shape[1]
    col_count = lax.axis_size("col")
    row_index = lax.axis_index(ROW)
    col_index = lax.axis_index("col")
    row_mask = listed_blocks(
        block_lists, block_counts, row_index * (row_cells // BLK), row_cells // BLK
    )
    col_mask = listed_blocks(
        block_lists, block_counts, col_index * (col_cells // BLK), col_cells // BLK
    )
    own_slot = l_store[0]
    chosen = (sibling_columns == col_index).astype(jnp.float32)
    placed = chosen[:, None, None] * own_slot[None]
    stacked = total_of(placed, "col")
    masked = stacked * row_mask[:, :, None]
    partial_value = (
        -jnp.einsum(
            "jrw,rc->jwc",
            masked,
            anc_inverse,
            precision=lax.Precision.HIGHEST,
            preferred_element_type=jnp.float32,
        )
        * col_mask[:, None, :]
    )
    upper_part = summed_rows(partial_value, ROW, 1)
    owner_table = (
        sibling_columns[:, None] == jnp.arange(col_count, dtype=jnp.int32)[None, :]
    ).astype(jnp.float32)
    slots = jnp.einsum(
        "jc,jwt->wct",
        owner_table,
        upper_part,
        precision=lax.Precision.HIGHEST,
        preferred_element_type=jnp.float32,
    )
    slots = slots.reshape(slots.shape[0], col_count * col_cells)
    by_owner = lax.all_to_all(slots, "col", split_axis=1, concat_axis=1, tiled=True)
    picked = lax.all_to_all(by_owner, ROW, split_axis=1, concat_axis=0, tiled=True)
    own_panel = jnp.sum(chosen[:, None, None] * masked, axis=0)
    inner_sum = jnp.dot(
        picked, own_panel, precision=lax.Precision.HIGHEST, preferred_element_type=jnp.float32
    )
    diag_total = nested_sum(inner_sum, ROW)
    present = jnp.sum(chosen)
    diag_out = (present * diag_inv[0] - diag_total)[None]
    lower_out = jnp.transpose(picked)[None]
    return (upper_part, lower_out, diag_out)


def solution(mesh):
    finer = Mesh(mesh.devices.reshape(8, 2, mesh.shape["col"]), ("row_0", "row_1", "col"))
    return jax.shard_map(
        per_device,
        mesh=finer,
        in_specs=(P(ROW, "col"), P("col", ROW, None), P("col", None, None), P(), P(), P()),
        out_specs=(P(None, ROW, "col"), P("col", ROW, None), P("col", None, None)),
        check_vma=False,
    )
```

profile of v0, /device:TPU:1, one launch (start us, length us, event | category | flops | bytes accessed | tf_op | source)
XLA Modules:
  0.0 358.0 jit_solution(242088408683245852)
XLA Ops:
  7.2 0.0 reduce-scatter.4.cloned.1.call-start
  7.2 1.3 fusion.15
  8.5 0.1 mul.66
  8.6 0.0 copy-start.3
  8.6 0.0 copy-start.2
  8.6 4.4 %bitcast_multiply_fusion = f32[5120,256]{1,0:T(8,128)} fusion(f32[1280,256]{1,0:T(8,128)} %bitcast.42, f32[5120]{0:T(1024)S(1)} %mul.67), kind=kLoop, calls=%fused_computation.2 | loop fusion | flops 1310720 | bytes 6574080 | tf_op jit(solution)/shard_map/mul | solution.py:86
  13.0 0.0 reduce-scatter.4.cloned.1.call-update
  13.0 0.0 all-gather.2.cloned.1.call-start
  13.1 71.6 %reduce-scatter.4.cloned.1.call-done = f32[320,256]{1,0:T(8,128)} async-done(((f32[5120,256]{1,0:T(8,128)}), f32[320,256]{1,0:T(8,128)}) %reduce-scatter.4.cloned.1.call-update) | async-done | bytes 327696 | tf_op jit(solution)/shard_map/reduce_scatter | solution.py:19
  84.7 0.0 all-gather.2.cloned.1.call-update
  84.7 0.0 reduce-scatter.6.cloned.1.call-start
  84.8 0.0 copy-done.3
  84.8 0.1 iota_compare_fusion.1
  84.9 0.0 copy-done.2
  84.9 0.5 and_reduce_fusion.1
  85.4 0.1 copy.32
  85.5 0.1 broadcast_bitcast_fusion.1
  85.6 0.1 copy.34
  85.7 0.1 broadcast_bitcast_fusion
  85.8 45.3 %all-gather.2.cloned.1.call-done = f32[5120,256]{1,0:T(8,128)} async-done(((f32[320,256]{1,0:T(8,128)}), f32[5120,256]{1,0:T(8,128)}) %all-gather.2.cloned.1.call-update) | async-done | bytes 5242896 | tf_op jit(solution)/shard_map/all_gather | solution.py:20
  131.1 28.0 %negate_multiply_fusion = f32[4,256,1280]{2,1,0:T(8,128)} fusion(f32[1280,1280]{1,0:T(8,128)} %param.6, f32[4,1280,256]{2,1,0:T(8,128)} %bitcast.40, f32[4,1280]{1,0:T(4,128)S(1)} %bitcast.46, f32[4,1280]{1,0:T(4,128)S(1)} %bitcast.44), kind=kOutput, calls=%fused_computation.4 | convolution fusion | flops 20136591360 | bytes 17080320 | tf_op jit(solution)/shard_map/jrw,rc->jwc/dot_general | solution.py:90
  159.1 0.0 copy-start.1
  159.1 0.0 reduce-scatter.6.cloned.1.call-update
  159.1 0.2 reduce-scatter.8.cloned.1.call-start
  159.3 65.1 %reduce-scatter.6.cloned.1.call-done = f32[4,32,1280]{2,1,0:T(8,128)} async-done(((f32[4,256,1280]{2,1,0:T(8,128)}), f32[4,32,1280]{2,1,0:T(8,128)}) %reduce-scatter.6.cloned.1.call-update) | async-done | bytes 655376 | tf_op jit(solution)/shard_map/reduce_scatter | solution.py:27
  224.4 0.0 reduce-scatter.8.cloned.1.call-update
  224.4 24.1 %reduce-scatter.8.cloned.1.call-done = f32[4,16,1280]{2,1,0:T(8,128)} async-done(((f32[4,32,1280]{2,1,0:T(8,128)}), f32[4,16,1280]{2,1,0:T(8,128)}) %reduce-scatter.8.cloned.1.call-update) | async-done | bytes 327696 | tf_op jit(solution)/shard_map/reduce_scatter | solution.py:27
  248.5 0.0 copy-done.1
  248.5 1.8 convolution_bitcast_fusion
  250.4 0.8 copy.36
  251.2 23.3 %all_to_all.32 = f32[16,16,1280]{2,0,1:T(8,128)} all-to-all(f32[16,16,1280]{2,0,1:T(8,128)S(1)} %copy.36), channel_id=1, replica_groups=mesh['row_0'=8,'row_1'=2,'col'=16] {'col'}, dimensions={1} | all-to-all | bytes 2621440 | tf_op jit(solution)/shard_map/all_to_all | solution.py:111
  274.4 8.3 %all-to-all-start.1 = ((f32[16,16,1280]{2,0,1:T(8,128)}), f32[16,16,1280]{2,0,1:T(8,128)S(1)}, u32[]{:S(2)}, u32[]{:S(2)}) async-start(f32[16,16,1280]{2,0,1:T(8,128)} %all_to_all.32), calls=%async_computation.4 | async-start | bytes 2621440 | tf_op jit(solution)/shard_map/all_to_all | solution.py:112
  282.7 0.0 copy-start
  282.7 3.1 multiply_reduce_fusion
  285.8 28.3 %all-to-all-done.1 = f32[16,16,1280]{2,0,1:T(8,128)S(1)} async-done(((f32[16,16,1280]{2,0,1:T(8,128)}), f32[16,16,1280]{2,0,1:T(8,128)S(1)}, u32[]{:S(2)}, u32[]{:S(2)}) %all-to-all-start.1) | async-done | bytes 1310752 | tf_op jit(solution)/shard_map/all_to_all | solution.py:112
  314.1 1.2 fusion.8
  315.3 19.5 %all_to_all.33 = f32[16,16,256]{2,1,0:T(8,128)S(1)} all-to-all(f32[16,16,256]{2,1,0:T(8,128)S(1)} %fusion.8), channel_id=1, replica_groups=mesh['row_0'=8,'row_1'=2,'col'=16] {'row_0','row_1'}, dimensions={0} | all-to-all | bytes 524288 | tf_op jit(solution)/shard_map/all_to_all | solution.py:54
  334.8 0.7 broadcast_in_dim.11
  335.5 3.5 all-to-all-start.3
  339.1 1.5 copy.37
  340.5 9.6 %all-to-all-done.3 = f32[16,16,256]{2,1,0:T(8,128)S(1)} async-done(((f32[16,16,256]{2,1,0:T(8,128)}), f32[16,16,256]{2,1,0:T(8,128)S(1)}, u32[]{:S(2)}, u32[]{:S(2)}) %all-to-all-start.3) | async-done | bytes 262176 | tf_op jit(solution)/shard_map/all_to_all | solution.py:39
  350.2 0.0 copy-done
  350.2 1.3 bitcast_subtract_fusion
  (7 shorter events, 0.1 us)
Async XLA Ops:
  7.2 77.5 %reduce-scatter.4.cloned.1.call-start = ((), (), s32[]{:S(2)}) async-start(), calls=%async_computation.7 | async-start | bytes 5570560 | tf_op jit(solution)/shard_map/reduce_scatter | solution.py:19
  8.6 76.2 %copy-start.3 = (s32[4]{0:T(128)S(1)}, s32[4]{0:T(128)}, u32[]{:S(2)}) copy-start(s32[4]{0:T(128)} %param.10) | copy-start | bytes 52
  8.6 76.3 %copy-start.2 = (s32[4,96]{1,0:T(4,128)S(1)}, s32[4,96]{1,0:T(4,128)}, u32[]{:S(2)}) copy-start(s32[4,96]{1,0:T(4,128)} %param.9) | copy-start | bytes 4612
  13.0 118.1 %all-gather.2.cloned.1.call-start = ((), (), s32[]{:S(2)}) async-start(), calls=%async_computation.8 | async-start | bytes 5570560 | tf_op jit(solution)/shard_map/all_gather | solution.py:20
  84.7 139.7 %reduce-scatter.6.cloned.1.call-start = ((), (), s32[]{:S(2)}) async-start(), calls=%async_computation.9 | async-start | bytes 5898240 | tf_op jit(solution)/shard_map/reduce_scatter | solution.py:27
  159.1 89.5 %copy-start.1 = (s32[4]{0:T(128)S(1)}, s32[4]{0:T(128)}, u32[]{:S(2)}) copy-start(s32[4]{0:T(128)} %param.11) | copy-start | bytes 52
  159.1 89.4 %reduce-scatter.8.cloned.1.call-start = ((), (), s32[]{:S(2)}) async-start(), calls=%async_computation.10 | async-start | bytes 983040 | tf_op jit(solution)/shard_map/reduce_scatter | solution.py:27
  274.4 39.7 %all-to-all-start.1 = ((f32[16,16,1280]{2,0,1:T(8,128)}), f32[16,16,1280]{2,0,1:T(8,128)S(1)}, u32[]{:S(2)}, u32[]{:S(2)}) async-start(f32[16,16,1280]{2,0,1:T(8,128)} %all_to_all.32), calls=%async_computation.4 | async-start | bytes 2621440 | tf_op jit(solution)/shard_map/all_to_all | solution.py:112
  282.7 67.4 %copy-start = (f32[1,256,256]{2,1,0:T(8,128)S(1)}, f32[1,256,256]{2,1,0:T(8,128)}, u32[]{:S(2)}) copy-start(f32[1,256,256]{2,1,0:T(8,128)} %param.8) | copy-start | bytes 786436
  335.5 14.6 %all-to-all-start.3 = ((f32[16,16,256]{2,1,0:T(8,128)}), f32[16,16,256]{2,1,0:T(8,128)S(1)}, u32[]{:S(2)}, u32[]{:S(2)}) async-start(f32[16,16,256]{2,1,0:T(8,128)} %broadcast_in_dim.11), calls=%async_computation.6 | async-start | bytes 524288 | tf_op jit(solution)/shard_map/all_to_all | solution.py:39
Sparse Core Ops, SparseCore 0:
  13.1 71.5 reduce-scatter.3
  86.5 44.4 all-gather.1
  159.2 65.1 reduce-scatter.5
  227.3 21.1 reduce-scatter.7
where the time goes:
time: 360 us; the launch traced here: 358 us
  waiting for transfers between devices  244 us (68%)
  blocking collectives  42.7 us (12%)
  matrix products  31.1 us (9%)
  between operations  13.9 us (4%)
  starting transfers between devices  12.2 us (3%)
  other arithmetic  10.7 us (3%)
    reduce_scatter x2, waiting for transfers between devices, summed_rows(): nearer = lax.psum_scatter(x, axes[0], scatter_dimension=dim, tiled=True)  89.2 us
    reduce_scatter x1, waiting for transfers between devices, total_of(): own = lax.psum_scatter(padded, axis, scatter_dimension=0, tiled=True)  71.6 us
    all_gather x1, waiting for transfers between devices, total_of(): whole = lax.all_gather(own, axis, axis=0, tiled=True)  45.3 us
    all_to_all x1, waiting for transfers between devices, per_device(): lax.all_to_all(by_owner, ROW, split_axis=1, concat_axis=0, tiled=True)  28.3 us
    dot_general x1, matrix products, per_device(): jnp.einsum('jrw,rc->jwc', masked, anc_inverse, precision=lax.Precision.HI...  28 us
    all_to_all x1, blocking collectives, per_device(): lax.all_to_all(slots, 'col', split_axis=1, concat_axis=1, tiled=True)  23.3 us
    all_to_all x1, blocking collectives, sum_at_owner(): parts = lax.all_to_all(cut_along(x, dim, length), axis, 0, 0, tiled=True)  19.5 us
    all_to_all x1, waiting for transfers between devices, from_everyone(): lax.all_to_all(jnp.broadcast_to(x[None], (length, *x.shape)), axis, 0, 0,...  9.61 us
  transfers between devices with their start and end apart: 6, of which 6 were waited for; matrix products, arithmetic and copies ran while one was open for 2% of the time, Pallas kernels for 0%

commit v1 on v0

v1 whole, which is shorter than its diff:
```python
import jax
import jax.numpy as jnp
from jax import lax
from jax.sharding import Mesh
from jax.sharding import PartitionSpec as P

BLK = 128
ROW = ("row_0", "row_1")


def listed_blocks(block_lists, block_counts, first_block, block_total):
    block_ids = first_block + jnp.arange(block_total, dtype=jnp.int32)
    valid_entry = jnp.arange(block_lists.shape[1], dtype=jnp.int32)[None, :] < block_counts[:, None]
    entry_hits = (block_lists[:, :, None] == block_ids[None, None, :]) & valid_entry[:, :, None]
    return jnp.repeat(jnp.any(entry_hits, axis=1).astype(jnp.float32), BLK, axis=1)


def summed_over(x, axis):
    parts = lax.all_to_all(x, axis, 0, 0, tiled=True)
    return jnp.sum(parts, axis=0)


def per_device(anc_inverse, l_store, diag_inv, block_lists, block_counts, sibling_columns):
    row_cells, col_cells = anc_inverse.shape
    width = l_store.shape[2]
    sib = sibling_columns.shape[0]
    n_col = lax.axis_size("col")
    n_row = lax.axis_size(ROW)
    row_index = lax.axis_index(ROW)
    col_index = lax.axis_index("col")
    row_mask = listed_blocks(
        block_lists, block_counts, row_index * (row_cells // BLK), row_cells // BLK
    )
    col_mask = listed_blocks(
        block_lists, block_counts, col_index * (col_cells // BLK), col_cells // BLK
    )
    own_slot = l_store[0]
    piece = row_cells // n_col
    scattered = lax.all_to_all(
        own_slot.reshape(n_col, piece, width), "col", 0, 0, tiled=True
    )
    owned = jnp.concatenate(
        [lax.dynamic_index_in_dim(scattered, sibling_columns[j], 0) for j in range(sib)]
    )
    panels = lax.all_gather(owned, "col", axis=0, tiled=False)
    masked = panels * row_mask.reshape(sib, n_col, piece).transpose(1, 0, 2)[..., None]
    partial_value = (
        -jnp.einsum(
            "pjrw,prc->jwc",
            masked,
            anc_inverse.reshape(n_col, piece, col_cells),
            precision=lax.Precision.HIGH,
            preferred_element_type=jnp.float32,
        )
        * col_mask[:, None, :]
    )
    nearer = lax.psum_scatter(partial_value, "row_0", scatter_dimension=1, tiled=True)
    upper_part = lax.psum_scatter(nearer, "row_1", scatter_dimension=1, tiled=True)
    slab = width // n_row
    swap = [
        (r * n_col + c, c * n_col + (r + c) % n_row) for r in range(n_row) for c in range(n_col)
    ]
    moved = lax.ppermute(upper_part, ROW + ("col",), swap)
    slots = jnp.zeros((n_col, slab, col_cells), jnp.float32)
    for j in range(sib):
        slots = lax.dynamic_update_slice_in_dim(slots, moved[j][None], sibling_columns[j], 0)
    gathered = lax.all_to_all(slots, "col", 0, 0, tiled=True)
    ordered = jnp.roll(gathered, -row_index, axis=0)
    picked = ordered.reshape(width, col_cells)
    chosen = (sibling_columns == col_index).astype(jnp.float32)
    own_mask = jnp.sum(chosen[:, None] * row_mask, axis=0)
    own_panel = own_slot * own_mask[:, None]
    inner_part = jnp.dot(
        picked, own_panel, precision=lax.Precision.HIGH, preferred_element_type=jnp.float32
    )
    own_rows = summed_over(inner_part.reshape(n_row, width // n_row, width), ROW)
    total = lax.all_to_all(
        jnp.broadcast_to(own_rows[None], (n_row, *own_rows.shape)), ROW, 0, 0, tiled=True
    )
    diag_total = total.reshape(width, width)
    present = jnp.sum(chosen)
    diag_out = (present * diag_inv[0] - diag_total)[None]
    lower_out = jnp.transpose(picked)[None]
    return (upper_part, lower_out, diag_out)


def solution(mesh):
    finer = Mesh(mesh.devices.reshape(8, 2, mesh.shape["col"]), ("row_0", "row_1", "col"))
    return jax.shard_map(
        per_device,
        mesh=finer,
        in_specs=(P(ROW, "col"), P("col", ROW, None), P("col", None, None), P(), P(), P()),
        out_specs=(P(None, ROW, "col"), P("col", ROW, None), P("col", None, None)),
        check_vma=False,
    )
```

time: 360 us -> 299 us (0.83)
  waiting for transfers between devices: 244 us -> 181 us
  starting transfers between devices: 12.2 us -> 44 us
  blocking collectives: 42.7 us -> 20.3 us
  matrix products: 31.1 us -> 18.4 us
  between operations: 13.9 us -> 21.4 us
  other arithmetic: 10.7 us -> 4.85 us
  local copies, waits for them, and re-layouts: 3.45 us -> 7.13 us
    reduce_scatter x3 -> x2, waiting for transfers between devices: 161 us -> 89.5 us  [the longest x1 65.3 us: per_device(): lax.psum_scatter(partial_value, 'row_0', scatter_dimension=1, tiled=True)]
    all_to_all x2 -> x3, starting transfers between devices: 11.8 us -> 42 us  [the longest x1 31.6 us: per_device(): gathered = lax.all_to_all(slots, 'col', 0, 0, tiled=True)]
    all_to_all x2 -> x1, blocking collectives: 42.7 us -> 20.3 us  [summed_over(): parts = lax.all_to_all(x, axis, 0, 0, tiled=True)]
    dot_general x3 -> x2, matrix products: 31.1 us -> 18.4 us  [the longest x1 17.6 us: per_device(): jnp.einsum('pjrw,prc->jwc', masked, anc_inverse.reshape(n_col, piece, col...]
    ppermute x0 -> x1, waiting for transfers between devices: none -> 11.7 us  [per_device(): moved = lax.ppermute(upper_part, ROW + ('col',), swap)]
    mul x1 -> x0, other arithmetic: 4.38 us -> none  [per_device(): placed = chosen[:, None, None] * own_slot[None]]
    all_to_all x2 -> x3, waiting for transfers between devices: 37.9 us -> 38.1 us  [the longest x1 18 us: per_device(): gathered = lax.all_to_all(slots, 'col', 0, 0, tiled=True)]
  transfers between devices with their start and end apart: 6 -> 7, of which waited for: 6 -> 7; matrix products, arithmetic and copies ran while one was open for 2% -> 1% of each run, Pallas kernels for 0% -> 0%
where the time goes in v1:
time: 299 us; the launch traced here: 297 us
  waiting for transfers between devices  181 us (61%)
  starting transfers between devices  44 us (15%)
  between operations  21.4 us (7%)
  blocking collectives  20.3 us (7%)
  matrix products  18.4 us (6%)
  local copies, waits for them, and re-layouts  7.13 us (2%)
  other arithmetic  4.85 us (2%)
    reduce_scatter x1, waiting for transfers between devices, per_device(): lax.psum_scatter(partial_value, 'row_0', scatter_dimension=1, tiled=True)  65.3 us
    all_gather x1, waiting for transfers between devices, per_device(): panels = lax.all_gather(owned, 'col', axis=0, tiled=False)  41.7 us
    all_to_all x1, starting transfers between devices, per_device(): gathered = lax.all_to_all(slots, 'col', 0, 0, tiled=True)  31.6 us
    reduce_scatter x1, waiting for transfers between devices, per_device(): lax.psum_scatter(nearer, 'row_1', scatter_dimension=1, tiled=True)  24.3 us
    all_to_all x1, blocking collectives, summed_over(): parts = lax.all_to_all(x, axis, 0, 0, tiled=True)  20.3 us
    all_to_all x1, waiting for transfers between devices, per_device(): gathered = lax.all_to_all(slots, 'col', 0, 0, tiled=True)  18 us
    dot_general x1, matrix products, per_device(): jnp.einsum('pjrw,prc->jwc', masked, anc_inverse.reshape(n_col, piece, col...  17.6 us
    ppermute x1, waiting for transfers between devices, per_device(): moved = lax.ppermute(upper_part, ROW + ('col',), swap)  11.7 us
  transfers between devices with their start and end apart: 7, of which 7 were waited for; matrix products, arithmetic and copies ran while one was open for 1% of the time, Pallas kernels for 0%

profile of v1, /device:TPU:1, one launch (start us, length us, event | category | flops | bytes accessed | tf_op | source)
XLA Modules:
  0.0 297.2 jit_solution(16738848684384025409)
XLA Ops:
  7.2 0.0 copy-start.2
  7.2 6.8 %all-to-all-start = ((f32[16,80,256]{2,1,0:T(8,128)}), f32[16,80,256]{2,1,0:T(8,128)S(1)}, u32[]{:S(2)}, u32[]{:S(2)}) async-start(f32[16,80,256]{2,1,0:T(8,128)} %bitcast.38), calls=%async_computation | async-start | bytes 2621440 | tf_op jit(solution)/shard_map/all_to_all | solution.py:39
  14.0 0.0 copy-start.4
  14.0 0.0 copy-start.3
  14.0 0.0 all-gather.3.cloned.1.call-start
  14.1 0.0 copy-done.2
  14.1 0.6 fusion.12
  22.2 10.5 %all-to-all-done = f32[16,80,256]{2,1,0:T(8,128)S(1)} async-done(((f32[16,80,256]{2,1,0:T(8,128)}), f32[16,80,256]{2,1,0:T(8,128)S(1)}, u32[]{:S(2)}, u32[]{:S(2)}) %all-to-all-start) | async-done | bytes 1310752 | tf_op jit(solution)/shard_map/all_to_all | solution.py:39
  32.7 0.7 pad_maximum_fusion
  33.5 0.0 all-gather.3.cloned.1.call-update
  33.5 0.0 reduce-scatter.3.cloned.1.call-start
  33.5 0.0 copy-done.4
  33.6 0.1 iota_compare_fusion
  33.6 0.0 copy-done.3
  33.6 0.5 and_reduce_fusion.1
  34.1 0.1 copy.18
  34.2 0.1 broadcast_in_dim.10
  34.3 0.1 reshape_reshape.3
  34.4 0.1 copy.20
  34.5 0.1 broadcast_bitcast_fusion
  34.6 41.7 %all-gather.3.cloned.1.call-done = f32[64,80,256]{2,1,0:T(8,128)} async-done(((f32[4,80,256]{2,1,0:T(8,128)}), f32[64,80,256]{2,1,0:T(8,128)}) %all-gather.3.cloned.1.call-update) | async-done | bytes 5242896 | tf_op jit(solution)/shard_map/all_gather | solution.py:45
  76.3 17.6 %fusion = f32[4,256,1280]{2,1,0:T(8,128)} fusion(f32[16,80,1280,1]{2,1,3,0:T(8,128)} %bitcast.42, f32[16,4,80,256]{3,2,1,0:T(8,128)} %bitcast.43, f32[4,1280]{1,0:T(4,128)S(1)} %bitcast.41, f32[16,4,80]{2,1,0:T(4,128)S(1)} %copy.19), kind=kOutput, calls=%fused_computation.1 | convolution fusion | flops 10070261760 | bytes 17080320 | tf_op jit(solution)/shard_map/pjrw,prc->jwc/dot_general | solution.py:48
  93.9 0.0 reduce-scatter.3.cloned.1.call-update
  93.9 0.0 reduce-scatter.5.cloned.1.call-start
  94.0 65.3 %reduce-scatter.3.cloned.1.call-done = f32[4,32,1280]{2,1,0:T(8,128)} async-done(((f32[4,256,1280]{2,1,0:T(8,128)}), f32[4,32,1280]{2,1,0:T(8,128)}) %reduce-scatter.3.cloned.1.call-update) | async-done | bytes 655376 | tf_op jit(solution)/shard_map/reduce_scatter | solution.py:57
  159.2 0.0 reduce-scatter.5.cloned.1.call-update
  159.3 24.3 %reduce-scatter.5.cloned.1.call-done = f32[4,16,1280]{2,1,0:T(8,128)} async-done(((f32[4,32,1280]{2,1,0:T(8,128)}), f32[4,16,1280]{2,1,0:T(8,128)}) %reduce-scatter.5.cloned.1.call-update) | async-done | bytes 327696 | tf_op jit(solution)/shard_map/reduce_scatter | solution.py:58
  183.5 1.9 collective-permute-start
  185.4 11.7 %collective-permute-done = f32[4,16,1280]{2,1,0:T(8,128)S(1)} collective-permute-done((f32[4,16,1280]{2,1,0:T(8,128)}, f32[4,16,1280]{2,1,0:T(8,128)S(1)}, u32[]{:S(2)}, u32[]{:S(2)}) %collective-permute-start) | collective-permute-done | bytes 327712 | tf_op jit(solution)/shard_map/ppermute | solution.py:63
  197.1 1.2 broadcast_in_dim.12
  198.3 0.6 slice_dynamic-update-slice_fusion.3
  199.0 0.6 slice_dynamic-update-slice_fusion.2
  199.6 0.6 slice_dynamic-update-slice_fusion.1
  200.3 0.6 slice_dynamic-update-slice_fusion
  200.9 31.6 %all-to-all-start.1 = ((f32[16,16,1280]{2,1,0:T(8,128)}), f32[16,16,1280]{2,1,0:T(8,128)}, u32[]{:S(2)}, u32[]{:S(2)}) async-start(f32[16,16,1280]{2,1,0:T(8,128)} %slice_dynamic-update-slice_fusion), calls=%async_computation.3 | async-start | bytes 2621440 | tf_op jit(solution)/shard_map/all_to_all | solution.py:67
  232.5 0.6 fusion.11
  233.1 0.1 select_reduce_fusion
  233.2 0.1 broadcast_bitcast_fusion.1
  233.3 0.0 copy-start
  233.3 18.0 %all-to-all-done.1 = f32[16,16,1280]{2,1,0:T(8,128)} async-done(((f32[16,16,1280]{2,1,0:T(8,128)}), f32[16,16,1280]{2,1,0:T(8,128)}, u32[]{:S(2)}, u32[]{:S(2)}) %all-to-all-start.1) | async-done | bytes 1310752 | tf_op jit(solution)/shard_map/all_to_all | solution.py:67
  251.3 1.5 fusion.6
  252.8 0.0 copy-done
  252.8 0.9 fusion.7
  253.7 20.3 %all_to_all.20 = f32[16,16,256]{2,1,0:T(8,128)S(1)} all-to-all(f32[16,16,256]{2,1,0:T(8,128)S(1)} %fusion.7), channel_id=1, replica_groups=mesh['row_0'=8,'row_1'=2,'col'=16] {'row_0','row_1'}, dimensions={0} | all-to-all | bytes 524288 | tf_op jit(solution)/shard_map/all_to_all | solution.py:19
  274.0 0.7 broadcast_in_dim.14
  274.7 3.5 %all-to-all-start.3 = ((f32[16,16,256]{2,1,0:T(8,128)}), f32[16,16,256]{2,1,0:T(8,128)S(1)}, u32[]{:S(2)}, u32[]{:S(2)}) async-start(f32[16,16,256]{2,1,0:T(8,128)} %broadcast_in_dim.14), calls=%async_computation.5 | async-start | bytes 524288 | tf_op jit(solution)/shard_map/all_to_all | solution.py:77
  278.3 0.0 copy-start.1
  278.3 1.5 copy.21
  279.7 9.6 %all-to-all-done.3 = f32[16,16,256]{2,1,0:T(8,128)S(1)} async-done(((f32[16,16,256]{2,1,0:T(8,128)}), f32[16,16,256]{2,1,0:T(8,128)S(1)}, u32[]{:S(2)}, u32[]{:S(2)}) %all-to-all-start.3) | async-done | bytes 262176 | tf_op jit(solution)/shard_map/all_to_all | solution.py:77
  289.3 0.0 copy-done.1
  289.3 1.3 bitcast_subtract_fusion
  (7 shorter events, 0.1 us)
Async XLA Ops:
  7.2 6.9 %copy-start.2 = (s32[4]{0:T(128)S(1)}, s32[4]{0:T(128)}, u32[]{:S(2)}) copy-start(s32[4]{0:T(128)} %param.11) | copy-start | bytes 52
  7.2 25.5 %all-to-all-start = ((f32[16,80,256]{2,1,0:T(8,128)}), f32[16,80,256]{2,1,0:T(8,128)S(1)}, u32[]{:S(2)}, u32[]{:S(2)}) async-start(f32[16,80,256]{2,1,0:T(8,128)} %bitcast.38), calls=%async_computation | async-start | bytes 2621440 | tf_op jit(solution)/shard_map/all_to_all | solution.py:39
  14.0 19.5 %copy-start.4 = (s32[4]{0:T(128)S(1)}, s32[4]{0:T(128)}, u32[]{:S(2)}) copy-start(s32[4]{0:T(128)} %param.10) | copy-start | bytes 52
  14.0 19.6 %copy-start.3 = (s32[4,96]{1,0:T(4,128)S(1)}, s32[4,96]{1,0:T(4,128)}, u32[]{:S(2)}) copy-start(s32[4,96]{1,0:T(4,128)} %param.9) | copy-start | bytes 4612
  14.0 62.3 %all-gather.3.cloned.1.call-start = ((), (), s32[]{:S(2)}) async-start(), calls=%async_computation.8 | async-start | bytes 5570560 | tf_op jit(solution)/shard_map/all_gather | solution.py:45
  33.5 125.8 %reduce-scatter.3.cloned.1.call-start = ((), (), s32[]{:S(2)}) async-start(), calls=%async_computation.6 | async-start | bytes 5898240 | tf_op jit(solution)/shard_map/reduce_scatter | solution.py:57
  93.9 89.6 %reduce-scatter.5.cloned.1.call-start = ((), (), s32[]{:S(2)}) async-start(), calls=%async_computation.7 | async-start | bytes 983040 | tf_op jit(solution)/shard_map/reduce_scatter | solution.py:58
  183.5 13.6 %collective-permute-start = (f32[4,16,1280]{2,1,0:T(8,128)}, f32[4,16,1280]{2,1,0:T(8,128)S(1)}, u32[]{:S(2)}, u32[]{:S(2)}) collective-permute-start(f32[4,16,1280]{2,1,0:T(8,128)} %reduce-scatter.5.cloned.1.call-done), channel_id=1, source_target_pairs={{0,0},{1,17},{2,34},{3,51},{4,68},{5,85},{6,102},{7,119},{8,136},{... | collective-permute-start | bytes 983048 | tf_op jit(solution)/shard_map/ppermute | solution.py:63
  200.9 50.4 %all-to-all-start.1 = ((f32[16,16,1280]{2,1,0:T(8,128)}), f32[16,16,1280]{2,1,0:T(8,128)}, u32[]{:S(2)}, u32[]{:S(2)}) async-start(f32[16,16,1280]{2,1,0:T(8,128)} %slice_dynamic-update-slice_fusion), calls=%async_computation.3 | async-start | bytes 2621440 | tf_op jit(solution)/shard_map/all_to_all | solution.py:67
  233.3 19.6 %copy-start = (f32[1,1280,256]{2,1,0:T(8,128)S(1)}, f32[1,1280,256]{2,1,0:T(8,128)}, u32[]{:S(2)}) copy-start(f32[1,1280,256]{2,1,0:T(8,128)} %param.7) | copy-start | bytes 3932164
  274.7 14.6 %all-to-all-start.3 = ((f32[16,16,256]{2,1,0:T(8,128)}), f32[16,16,256]{2,1,0:T(8,128)S(1)}, u32[]{:S(2)}, u32[]{:S(2)}) async-start(f32[16,16,256]{2,1,0:T(8,128)} %broadcast_in_dim.14), calls=%async_computation.5 | async-start | bytes 524288 | tf_op jit(solution)/shard_map/all_to_all | solution.py:77
  278.3 11.1 %copy-start.1 = (f32[1,256,256]{2,1,0:T(8,128)S(1)}, f32[1,256,256]{2,1,0:T(8,128)}, u32[]{:S(2)}) copy-start(f32[1,256,256]{2,1,0:T(8,128)} %param.8) | copy-start | bytes 786436
Sparse Core Ops, SparseCore 0:
  33.6 42.6 all-gather.2
  94.1 65.1 reduce-scatter.2
  162.3 21.1 reduce-scatter.4

commit v2 on v1

--- a/solution.py
+++ b/solution.py
@@ -15,9 +15,9 @@
     return jnp.repeat(jnp.any(entry_hits, axis=1).astype(jnp.float32), BLK, axis=1)
 
 
-def summed_over(x, axis):
-    parts = lax.all_to_all(x, axis, 0, 0, tiled=True)
-    return jnp.sum(parts, axis=0)
+def swapped(x, axis, bit):
+    length = lax.axis_size(axis)
+    return lax.ppermute(x, axis, [(i, i ^ bit) for i in range(length)])
 
 
 def per_device(anc_inverse, l_store, diag_inv, block_lists, block_counts, sibling_columns):
@@ -55,32 +55,39 @@
         * col_mask[:, None, :]
     )
     nearer = lax.psum_scatter(partial_value, "row_0", scatter_dimension=1, tiled=True)
-    upper_part = lax.psum_scatter(nearer, "row_1", scatter_dimension=1, tiled=True)
     slab = width // n_row
-    swap = [
-        (r * n_col + c, c * n_col + (r + c) % n_row) for r in range(n_row) for c in range(n_col)
-    ]
-    moved = lax.ppermute(upper_part, ROW + ("col",), swap)
-    slots = jnp.zeros((n_col, slab, col_cells), jnp.float32)
+    half = lax.axis_index("row_1")
+    sent = lax.dynamic_slice_in_dim(nearer, (1 - half) * slab, slab, 1)
+    kept = lax.dynamic_slice_in_dim(nearer, half * slab, slab, 1)
+    upper_part = kept + swapped(sent, "row_1", 1)
+    by_width = lax.all_to_all(upper_part.transpose(1, 0, 2), "col", 0, 0, tiled=True)
+    moved = lax.all_to_all(by_width, ROW, 0, 0, tiled=True)
+    slots = jnp.zeros((n_col, n_row, col_cells), jnp.float32)
     for j in range(sib):
-        slots = lax.dynamic_update_slice_in_dim(slots, moved[j][None], sibling_columns[j], 0)
+        slots = lax.dynamic_update_slice_in_dim(slots, moved[None, :, j], sibling_columns[j], 0)
     gathered = lax.all_to_all(slots, "col", 0, 0, tiled=True)
-    ordered = jnp.roll(gathered, -row_index, axis=0)
-    picked = ordered.reshape(width, col_cells)
-    chosen = (sibling_columns == col_index).astype(jnp.float32)
-    own_mask = jnp.sum(chosen[:, None] * row_mask, axis=0)
-    own_panel = own_slot * own_mask[:, None]
-    inner_part = jnp.dot(
-        picked, own_panel, precision=lax.Precision.HIGH, preferred_element_type=jnp.float32
+    whole_panels = masked.transpose(1, 0, 2, 3).reshape(sib, row_cells, width)
+    inner = jnp.einsum(
+        "rjt,jtv->jrv",
+        moved,
+        whole_panels,
+        precision=lax.Precision.HIGH,
+        preferred_element_type=jnp.float32,
     )
-    own_rows = summed_over(inner_part.reshape(n_row, width // n_row, width), ROW)
-    total = lax.all_to_all(
-        jnp.broadcast_to(own_rows[None], (n_row, *own_rows.shape)), ROW, 0, 0, tiled=True
-    )
-    diag_total = total.reshape(width, width)
-    present = jnp.sum(chosen)
+    inner = inner + swapped(inner, "row_1", 1)
+    for step in (1, 2, 4):
+        inner = inner + swapped(inner, "row_0", step)
+    gathered, inner = lax.optimization_barrier((gathered, inner))
+    diag_slots = jnp.zeros((n_col, n_row, width), jnp.float32)
+    for j in range(sib):
+        diag_slots = lax.dynamic_update_slice_in_dim(
+            diag_slots, inner[j][None], sibling_columns[j], 0
+        )
+    diag_parts = lax.all_to_all(diag_slots, "col", 0, 0, tiled=True)
+    lower_out = gathered.transpose(2, 1, 0).reshape(1, row_cells, width)
+    diag_total = diag_parts.transpose(1, 0, 2).reshape(width, width)
+    present = jnp.sum((sibling_columns == col_index).astype(jnp.float32))
     diag_out = (present * diag_inv[0] - diag_total)[None]
-    lower_out = jnp.transpose(picked)[None]
     return (upper_part, lower_out, diag_out)
 
 

time: 299 us -> 276 us (0.923)
  waiting for transfers between devices: 181 us -> 151 us
  starting transfers between devices: 44 us -> 28.7 us
  blocking collectives: 20.3 us -> 33 us
  local copies, waits for them, and re-layouts: 7.13 us -> 13.1 us
  other arithmetic: 4.85 us -> 8.57 us
    all_to_all x1, starting transfers between devices: 31.6 us -> 6.46 us  [per_device(): gathered = lax.all_to_all(slots, 'col', 0, 0, tiled=True)]
    reduce_scatter x1 -> x0, waiting for transfers between devices: 24.3 us -> none  [per_device(): lax.psum_scatter(nearer, 'row_1', scatter_dimension=1, tiled=True)]
    ppermute x1 -> x5, waiting for transfers between devices: 11.7 us -> 30.9 us  [swapped(): return lax.ppermute(x, axis, [(i, i ^ bit) for i in range(length)])]
    all_to_all x1, waiting for transfers between devices: 18 us -> 0.01 us  [per_device(): gathered = lax.all_to_all(slots, 'col', 0, 0, tiled=True)]
    all_to_all x1 -> x2, blocking collectives: 20.3 us -> 33 us  [the longest x1 18.9 us: per_device(): moved = lax.all_to_all(by_width, ROW, 0, 0, tiled=True)]
    all_to_all x1, starting transfers between devices: 3.53 us -> 9.51 us  [per_device(): diag_parts = lax.all_to_all(diag_slots, 'col', 0, 0, tiled=True)]
    all_to_all x1, waiting for transfers between devices: 9.6 us -> 4.34 us  [per_device(): diag_parts = lax.all_to_all(diag_slots, 'col', 0, 0, tiled=True)]
    ppermute x1 -> x5, starting transfers between devices: 1.91 us -> 5.84 us  [swapped(): return lax.ppermute(x, axis, [(i, i ^ bit) for i in range(length)])]
  transfers between devices with their start and end apart: 7 -> 10, of which waited for: 7 -> 9; matrix products, arithmetic and copies ran while one was open for 1% -> 4% of each run, Pallas kernels for 0% -> 0%
where the time goes in v2:
time: 276 us; the launch traced here: 275 us
  waiting for transfers between devices  151 us (55%)
  blocking collectives  33 us (12%)
  starting transfers between devices  28.7 us (10%)
  between operations  21.7 us (8%)
  matrix products  19.2 us (7%)
  local copies, waits for them, and re-layouts  13.1 us (5%)
  other arithmetic  8.57 us (3%)
    reduce_scatter x1, waiting for transfers between devices, per_device(): lax.psum_scatter(partial_value, 'row_0', scatter_dimension=1, tiled=True)  65.3 us
    all_gather x1, waiting for transfers between devices, per_device(): panels = lax.all_gather(owned, 'col', axis=0, tiled=False)  40.4 us
    ppermute x5, waiting for transfers between devices, swapped(): return lax.ppermute(x, axis, [(i, i ^ bit) for i in range(length)])  30.9 us
    all_to_all x1, blocking collectives, per_device(): moved = lax.all_to_all(by_width, ROW, 0, 0, tiled=True)  18.9 us
    dot_general x1, matrix products, per_device(): jnp.einsum('pjrw,prc->jwc', masked, anc_inverse.reshape(n_col, piece, col...  17.6 us
    all_to_all x1, blocking collectives, per_device(): lax.all_to_all(upper_part.transpose(1, 0, 2), 'col', 0, 0, tiled=True)  14.1 us
    all_to_all x1, waiting for transfers between devices, per_device(): lax.all_to_all(own_slot.reshape(n_col, piece, width), 'col', 0, 0, tiled=...  9.71 us
    all_to_all x1, starting transfers between devices, per_device(): diag_parts = lax.all_to_all(diag_slots, 'col', 0, 0, tiled=True)  9.51 us
  transfers between devices with their start and end apart: 10, of which 9 were waited for; matrix products, arithmetic and copies ran while one was open for 4% of the time, Pallas kernels for 0%

profile of v2, /device:TPU:1, one launch (start us, length us, event | category | flops | bytes accessed | tf_op | source)
XLA Modules:
  0.0 274.9 jit_solution(12878188339012693242)
XLA Ops:
  7.2 6.8 %all-to-all-start = ((f32[16,80,256]{2,1,0:T(8,128)}), f32[16,80,256]{2,1,0:T(8,128)S(1)}, u32[]{:S(2)}, u32[]{:S(2)}) async-start(f32[16,80,256]{2,1,0:T(8,128)} %bitcast.47), calls=%async_computation | async-start | bytes 2621440 | tf_op jit(solution)/shard_map/all_to_all | solution.py:39
  14.0 0.0 all-gather.3.cloned.1.call-start
  14.0 1.4 fusion.9
  23.0 9.7 %all-to-all-done = f32[16,80,256]{2,1,0:T(8,128)S(1)} async-done(((f32[16,80,256]{2,1,0:T(8,128)}), f32[16,80,256]{2,1,0:T(8,128)S(1)}, u32[]{:S(2)}, u32[]{:S(2)}) %all-to-all-start) | async-done | bytes 1310752 | tf_op jit(solution)/shard_map/all_to_all | solution.py:39
  32.7 0.7 pad_maximum_fusion
  33.4 0.0 all-gather.3.cloned.1.call-update
  33.5 0.0 reduce-scatter.2.cloned.1.call-start
  33.5 0.7 iota_compare_fusion
  34.3 1.2 and_reduce_fusion.1
  35.4 0.1 copy.67
  35.6 0.1 broadcast_bitcast_fusion
  35.7 0.1 copy.65
  35.8 0.1 broadcast_in_dim.8
  35.8 0.1 reshape_reshape.3
  35.9 40.4 %all-gather.3.cloned.1.call-done = f32[64,80,256]{2,1,0:T(8,128)} async-done(((f32[4,80,256]{2,1,0:T(8,128)}), f32[64,80,256]{2,1,0:T(8,128)}) %all-gather.3.cloned.1.call-update) | async-done | bytes 5242896 | tf_op jit(solution)/shard_map/all_gather | solution.py:45
  76.3 17.6 %fusion = f32[4,256,1280]{2,1,0:T(8,128)} fusion(f32[16,80,1280,1]{2,1,3,0:T(8,128)} %bitcast.50, f32[16,4,80,256]{3,2,1,0:T(8,128)} %bitcast.43, f32[4,1280]{1,0:T(4,128)S(1)} %bitcast.49, f32[16,4,80]{2,1,0:T(4,128)S(1)} %copy.66), kind=kOutput, calls=%fused_computation.1 | convolution fusion | flops 10070261760 | bytes 17080320 | tf_op jit(solution)/shard_map/pjrw,prc->jwc/dot_general | solution.py:48
  93.9 0.0 reduce-scatter.2.cloned.1.call-update
  93.9 65.3 %reduce-scatter.2.cloned.1.call-done = f32[4,32,1280]{2,1,0:T(8,128)} async-done(((f32[4,256,1280]{2,1,0:T(8,128)}), f32[4,32,1280]{2,1,0:T(8,128)}) %reduce-scatter.2.cloned.1.call-update) | async-done | bytes 655376 | tf_op jit(solution)/shard_map/reduce_scatter | solution.py:57
  159.2 1.0 constant_dynamic-slice_fusion
  160.2 2.8 %collective-permute-start = (f32[4,16,1280]{2,1,0:T(8,128)S(1)}, f32[4,16,1280]{2,1,0:T(8,128)S(1)}, u32[]{:S(2)}, u32[]{:S(2)}) collective-permute-start(f32[4,16,1280]{2,1,0:T(8,128)S(1)} %constant_dynamic-slice_fusion), channel_id=1, source_target_pairs={{0,16},{16,0},{1,17},{17,1},{2,18},{18,2},{3,19},{19,3},{4,20},{20... | collective-permute-start | bytes 983048 | tf_op jit(solution)/shard_map/ppermute | solution.py:20
  163.0 7.4 %collective-permute-done = f32[4,16,1280]{2,1,0:T(8,128)S(1)} collective-permute-done((f32[4,16,1280]{2,1,0:T(8,128)S(1)}, f32[4,16,1280]{2,1,0:T(8,128)S(1)}, u32[]{:S(2)}, u32[]{:S(2)}) %collective-permute-start) | collective-permute-done | bytes 327712 | tf_op jit(solution)/shard_map/ppermute | solution.py:20
  170.5 1.0 dynamic-slice_add_fusion
  171.5 0.0 copy-start
  171.5 0.2 copy.68
  171.7 14.1 %all_to_all.25 = f32[16,4,1280]{2,1,0:T(4,128)S(1)} all-to-all(f32[16,4,1280]{2,1,0:T(4,128)S(1)} %copy.68), channel_id=1, replica_groups=mesh['row_0'=8,'row_1'=2,'col'=16] {'col'}, dimensions={0} | all-to-all | bytes 655360 | tf_op jit(solution)/shard_map/all_to_all | solution.py:63
  185.8 18.9 %all_to_all.26 = f32[16,4,1280]{2,1,0:T(4,128)S(1)} all-to-all(f32[16,4,1280]{2,1,0:T(4,128)S(1)} %all_to_all.25), channel_id=1, replica_groups=mesh['row_0'=8,'row_1'=2,'col'=16] {'row_0','row_1'}, dimensions={0} | all-to-all | bytes 655360 | tf_op jit(solution)/shard_map/all_to_all | solution.py:64
  204.6 0.2 slice_bitcast_fusion
  204.9 1.2 broadcast_in_dim.10
  206.1 0.6 copy_dynamic-update-slice_fusion.3
  206.7 0.6 copy_dynamic-update-slice_fusion.2
  207.4 0.6 copy_dynamic-update-slice_fusion.1
  208.0 0.6 copy_dynamic-update-slice_fusion
  208.6 6.5 %all-to-all-start.3 = ((f32[16,16,1280]{2,1,0:T(8,128)}), f32[16,16,1280]{2,1,0:T(8,128)S(1)}, u32[]{:S(2)}, u32[]{:S(2)}) async-start(f32[16,16,1280]{2,1,0:T(8,128)} %copy_dynamic-update-slice_fusion), calls=%async_computation.4 | async-start | bytes 2621440 | tf_op jit(solution)/shard_map/all_to_all | solution.py:68
  215.1 3.0 %multiply_bitcast_fusion = f32[4,16,80,256]{3,2,0,1:T(8,128)S(1)} fusion(f32[16,4,80,256]{3,2,1,0:T(8,128)} %bitcast.44, f32[16,4,80]{2,1,0:T(4,128)S(1)} %copy.66), kind=kLoop, calls=%fused_computation.2 | loop fusion | flops 1310720 | bytes 10506240 | tf_op jit(solution)/shard_map/transpose | solution.py:69
  218.1 0.0 copy-done
  218.1 0.5 copy.73
  218.5 0.0 copy-start.2
  218.6 0.0 copy-start.1
  218.6 1.7 fusion.6
  220.2 0.6 collective-permute-start.1
  220.8 10.0 %collective-permute-done.1 = f32[4,16,256]{2,1,0:T(8,128)S(1)} collective-permute-done((f32[4,16,256]{2,1,0:T(8,128)S(1)}, f32[4,16,256]{2,1,0:T(8,128)S(1)}, u32[]{:S(2)}, u32[]{:S(2)}) %collective-permute-start.1) | collective-permute-done | bytes 65568 | tf_op jit(solution)/shard_map/ppermute | solution.py:20
  230.8 0.3 collective-permute-start.2
  231.1 3.1 %collective-permute-done.2 = f32[4,16,256]{2,1,0:T(8,128)S(1)} collective-permute-done((f32[4,16,256]{2,1,0:T(8,128)S(1)}, f32[4,16,256]{2,1,0:T(8,128)S(1)}, u32[]{:S(2)}, u32[]{:S(2)}) %collective-permute-start.2) | collective-permute-done | bytes 65568 | tf_op jit(solution)/shard_map/ppermute | solution.py:20
  234.2 1.0 collective-permute-start.3
  235.1 3.8 %collective-permute-done.3 = f32[4,16,256]{2,1,0:T(8,128)S(1)} collective-permute-done((f32[4,16,256]{2,1,0:T(8,128)S(1)}, f32[4,16,256]{2,1,0:T(8,128)S(1)}, u32[]{:S(2)}, u32[]{:S(2)}) %collective-permute-start.3) | collective-permute-done | bytes 65568 | tf_op jit(solution)/shard_map/ppermute | solution.py:20
  238.9 1.2 collective-permute-start.4
  240.2 6.6 %collective-permute-done.4 = f32[4,16,256]{2,1,0:T(8,128)S(1)} collective-permute-done((f32[4,16,256]{2,1,0:T(8,128)S(1)}, f32[4,16,256]{2,1,0:T(8,128)S(1)}, u32[]{:S(2)}, u32[]{:S(2)}) %collective-permute-start.4) | collective-permute-done | bytes 65568 | tf_op jit(solution)/shard_map/ppermute | solution.py:20
  246.8 0.0 all-to-all-done.3
  246.8 0.7 broadcast_in_dim.11
  247.5 0.6 slice_dynamic-update-slice_fusion.3
  248.1 0.6 slice_dynamic-update-slice_fusion.2
  248.7 0.6 slice_dynamic-update-slice_fusion.1
  249.3 0.6 slice_dynamic-update-slice_fusion
  249.9 9.5 %all-to-all-start.4 = ((f32[16,16,256]{2,1,0:T(8,128)}), f32[16,16,256]{2,1,0:T(8,128)S(1)}, u32[]{:S(2)}, u32[]{:S(2)}) async-start(f32[16,16,256]{2,1,0:T(8,128)} %slice_dynamic-update-slice_fusion), calls=%async_computation.5 | async-start | bytes 524288 | tf_op jit(solution)/shard_map/all_to_all | solution.py:86
  259.4 0.0 copy-done.2
  259.4 0.6 fusion.8
  260.1 0.8 copy.75
  260.8 1.5 copy.77
  262.3 4.3 %all-to-all-done.4 = f32[16,16,256]{2,1,0:T(8,128)S(1)} async-done(((f32[16,16,256]{2,1,0:T(8,128)}), f32[16,16,256]{2,1,0:T(8,128)S(1)}, u32[]{:S(2)}, u32[]{:S(2)}) %all-to-all-start.4) | async-done | bytes 262176 | tf_op jit(solution)/shard_map/all_to_all | solution.py:86
  266.6 0.2 copy.76
  266.8 0.0 copy-done.1
  266.8 1.3 bitcast_subtract_fusion
  (10 shorter events, 0.1 us)
Async XLA Ops:
  7.2 25.5 %all-to-all-start = ((f32[16,80,256]{2,1,0:T(8,128)}), f32[16,80,256]{2,1,0:T(8,128)S(1)}, u32[]{:S(2)}, u32[]{:S(2)}) async-start(f32[16,80,256]{2,1,0:T(8,128)} %bitcast.47), calls=%async_computation | async-start | bytes 2621440 | tf_op jit(solution)/shard_map/all_to_all | solution.py:39
  14.0 62.3 %all-gather.3.cloned.1.call-start = ((), (), s32[]{:S(2)}) async-start(), calls=%async_computation.7 | async-start | bytes 5570560 | tf_op jit(solution)/shard_map/all_gather | solution.py:45
  33.5 125.7 %reduce-scatter.2.cloned.1.call-start = ((), (), s32[]{:S(2)}) async-start(), calls=%async_computation.6 | async-start | bytes 5898240 | tf_op jit(solution)/shard_map/reduce_scatter | solution.py:57
  160.2 10.2 %collective-permute-start = (f32[4,16,1280]{2,1,0:T(8,128)S(1)}, f32[4,16,1280]{2,1,0:T(8,128)S(1)}, u32[]{:S(2)}, u32[]{:S(2)}) collective-permute-start(f32[4,16,1280]{2,1,0:T(8,128)S(1)} %constant_dynamic-slice_fusion), channel_id=1, source_target_pairs={{0,16},{16,0},{1,17},{17,1},{2,18},{18,2},{3,19},{19,3},{4,20},{20... | collective-permute-start | bytes 983048 | tf_op jit(solution)/shard_map/ppermute | solution.py:20
  171.5 46.6 %copy-start = (f32[4,16,1280]{2,1,0:T(8,128)}, f32[4,16,1280]{2,1,0:T(8,128)S(1)}, u32[]{:S(2)}) copy-start(f32[4,16,1280]{2,1,0:T(8,128)S(1)} %dynamic-slice_add_fusion) | copy-start | bytes 983044
  208.6 38.1 %all-to-all-start.3 = ((f32[16,16,1280]{2,1,0:T(8,128)}), f32[16,16,1280]{2,1,0:T(8,128)S(1)}, u32[]{:S(2)}, u32[]{:S(2)}) async-start(f32[16,16,1280]{2,1,0:T(8,128)} %copy_dynamic-update-slice_fusion), calls=%async_computation.4 | async-start | bytes 2621440 | tf_op jit(solution)/shard_map/all_to_all | solution.py:68
  218.5 40.9 %copy-start.2 = (s32[4]{0:T(128)S(1)}, s32[4]{0:T(128)}, u32[]{:S(2)}) copy-start(s32[4]{0:T(128)} %param.11) | copy-start | bytes 52
  218.6 48.2 %copy-start.1 = (f32[1,256,256]{2,1,0:T(8,128)S(1)}, f32[1,256,256]{2,1,0:T(8,128)}, u32[]{:S(2)}) copy-start(f32[1,256,256]{2,1,0:T(8,128)} %param.8) | copy-start | bytes 786436
  220.2 10.6 %collective-permute-start.1 = (f32[4,16,256]{2,1,0:T(8,128)S(1)}, f32[4,16,256]{2,1,0:T(8,128)S(1)}, u32[]{:S(2)}, u32[]{:S(2)}) collective-permute-start(f32[4,16,256]{2,1,0:T(8,128)S(1)} %fusion.6), channel_id=1, source_target_pairs={{0,16},{16,0},{1,17},{17,1},{2,18},{18,2},{3,19},{19,3},{4,20},{20... | collective-permute-start | bytes 196616 | tf_op jit(solution)/shard_map/ppermute | solution.py:20
  230.8 3.3 %collective-permute-start.2 = (f32[4,16,256]{2,1,0:T(8,128)S(1)}, f32[4,16,256]{2,1,0:T(8,128)S(1)}, u32[]{:S(2)}, u32[]{:S(2)}) collective-permute-start(f32[4,16,256]{2,1,0:T(8,128)S(1)} %add.79), channel_id=1, source_target_pairs={{0,32},{32,0},{64,96},{96,64},{128,160},{160,128},{192,224},{224,1... | collective-permute-start | bytes 196616 | tf_op jit(solution)/shard_map/ppermute | solution.py:20
  234.2 4.7 %collective-permute-start.3 = (f32[4,16,256]{2,1,0:T(8,128)S(1)}, f32[4,16,256]{2,1,0:T(8,128)S(1)}, u32[]{:S(2)}, u32[]{:S(2)}) collective-permute-start(f32[4,16,256]{2,1,0:T(8,128)S(1)} %add.80), channel_id=1, source_target_pairs={{0,64},{32,96},{64,0},{96,32},{128,192},{160,224},{192,128},{224,1... | collective-permute-start | bytes 196616 | tf_op jit(solution)/shard_map/ppermute | solution.py:20
  238.9 7.8 %collective-permute-start.4 = (f32[4,16,256]{2,1,0:T(8,128)S(1)}, f32[4,16,256]{2,1,0:T(8,128)S(1)}, u32[]{:S(2)}, u32[]{:S(2)}) collective-permute-start(f32[4,16,256]{2,1,0:T(8,128)S(1)} %add.81), channel_id=1, source_target_pairs={{0,128},{32,160},{64,192},{96,224},{128,0},{160,32},{192,64},{224,... | collective-permute-start | bytes 196616 | tf_op jit(solution)/shard_map/ppermute | solution.py:20
  249.9 16.7 %all-to-all-start.4 = ((f32[16,16,256]{2,1,0:T(8,128)}), f32[16,16,256]{2,1,0:T(8,128)S(1)}, u32[]{:S(2)}, u32[]{:S(2)}) async-start(f32[16,16,256]{2,1,0:T(8,128)} %slice_dynamic-update-slice_fusion), calls=%async_computation.5 | async-start | bytes 524288 | tf_op jit(solution)/shard_map/all_to_all | solution.py:86
Sparse Core Ops, SparseCore 0:
  33.6 42.6 all-gather.2
  94.0 65.1 reduce-scatter.1

commit v3 on v2

v3 whole, which is shorter than its diff:
```python
import functools

import jax
import jax.numpy as jnp
from jax import lax
from jax.experimental import pallas as pl
from jax.experimental.pallas import tpu as pltpu
from jax.sharding import Mesh
from jax.sharding import PartitionSpec as P

BLK = 128
SUB = 8
ROW = ("row_0", "row_1")
COL = ("col_y", "col_x", "core")
CAPS = (28,)

ROW_BLOCK, ROW_START, COL_BLOCK, COL_START = 0, 64, 72, 136
PIECE, ROW_SLOT, COL_SLOT, SOURCE, HALF, TABLE = 144, 160, 224, 288, 352, 360

SMEM = pl.BlockSpec(memory_space=pltpu.SMEM)
VMEM = pl.BlockSpec(memory_space=pltpu.VMEM)


def swapped(x, axis, bit):
    length = lax.axis_size(axis)
    return lax.ppermute(x, axis, [(i, i ^ bit) for i in range(length)])


def turned(x, axis, shift):
    length = lax.axis_size(axis)
    return lax.ppermute(x, axis, [(i, (i + shift) % length) for i in range(length)])


def member_blocks(block_lists, block_counts, block_total):
    block_ids = jnp.arange(block_total, dtype=jnp.int32)
    valid_entry = jnp.arange(block_lists.shape[1], dtype=jnp.int32)[None, :] < block_counts[:, None]
    entry_hits = (block_lists[:, :, None] == block_ids[None, None, :]) & valid_entry[:, :, None]
    return jnp.any(entry_hits, axis=1).astype(jnp.int32)


def slot_tables(listed):
    sib, blocks = listed.shape
    flat = listed.reshape(-1)
    place = jnp.arange(sib * blocks, dtype=jnp.int32)
    before = jnp.sum(jnp.where(place[None, :] < place[:, None], flat[None, :], 0), axis=1)
    here = (before[None, :] == place[:, None]) & (flat[None, :] > 0)
    code = jnp.sum(jnp.where(here, place[None, :], 0), axis=1)
    bounds = jnp.arange(sib + 1, dtype=jnp.int32) * blocks
    start = jnp.sum(jnp.where(place[None, :] < bounds[:, None], flat[None, :], 0), axis=1)
    slot = jnp.where(flat > 0, before, -1)
    return code, start, slot


def padded(values, length):
    return jnp.pad(values.astype(jnp.int32), (0, length - values.shape[0]))


def pick_kernel(cap, tab, x_ref, o_ref):
    for q in range(cap):
        o_ref[q] = x_ref[tab[SOURCE + q]]


def product_kernel(cap, sib, tab, g0, g1, c0, c1, ah, al, u_ref, p_ref, lhs, acc):
    parts = (g0, g1, c0, c1)
    for i in range(4 * len(parts)):
        at = pl.multiple_of(tab[PIECE + i] * SUB, SUB)
        p_ref[:, pl.ds(at, SUB), :] = parts[i // 4][i % 4]
    chunks, _, rows, _ = u_ref.shape

    def tile(ref, b, t):
        return ref[
            pl.ds(pl.multiple_of(b * BLK, BLK), BLK), pl.ds(pl.multiple_of(t * BLK, BLK), BLK)
        ]

    def square(ref, b0, b1, t0, t1):
        top = jnp.concatenate([tile(ref, b0, t0), tile(ref, b0, t1)], axis=1)
        low = jnp.concatenate([tile(ref, b1, t0), tile(ref, b1, t1)], axis=1)
        return jnp.concatenate([top, low], axis=0)

    for j in range(sib):
        r0 = tab[ROW_START + j]
        r1 = tab[ROW_START + j + 1]
        n0 = tab[COL_START + j]
        n1 = tab[COL_START + j + 1]
        pairs = (r1 - r0 + 1) // 2

        def split(i, carry, r0=r0, r1=r1):
            q = r0 + 2 * i
            second = jnp.where(q + 1 < r1, p_ref[jnp.minimum(q + 1, cap - 1)], 0.0)
            block = jnp.concatenate([p_ref[q], second], axis=0).T
            hi = block.astype(jnp.bfloat16)
            lo = (block - hi.astype(jnp.float32)).astype(jnp.bfloat16)
            lhs[i] = jnp.concatenate([hi, hi, lo], axis=1)
            return carry

        lax.fori_loop(0, pairs, split, 0)

        def columns(o, carry, r0=r0, n0=n0, n1=n1, pairs=pairs):
            s = n0 + 2 * o
            t0 = tab[COL_BLOCK + s]
            t1 = tab[COL_BLOCK + s + 1]
            acc[...] = jnp.zeros_like(acc)

            def rows_of(i, inner):
                b0 = tab[ROW_BLOCK + r0 + 2 * i]
                b1 = tab[ROW_BLOCK + r0 + 2 * i + 1]
                hi = square(ah, b0, b1, t0, t1)
                lo = square(al, b0, b1, t0, t1)
                acc[...] += jnp.dot(
                    lhs[i],
                    jnp.concatenate([hi, lo, hi], axis=0),
                    preferred_element_type=jnp.float32,
                )
                return inner

            lax.fori_loop(0, pairs, rows_of, 0)
            for z in range(chunks):
                u_ref[z, s] = -acc[z * rows : (z + 1) * rows, :BLK]

            @pl.when(s + 1 < n1)
            def _():
                for z in range(chunks):
                    u_ref[z, s + 1] = -acc[z * rows : (z + 1) * rows, BLK:]

            return carry

        lax.fori_loop(0, (n1 - n0 + 1) // 2, columns, 0)

    def clear(s, carry):
        u_ref[:, s] = jnp.zeros((chunks, rows, BLK), jnp.float32)
        return carry

    lax.fori_loop(tab[COL_START + sib], cap, clear, 0)


def spread_kernel(tab, p_ref, o_ref):
    def one(i, carry):
        slot = tab[ROW_SLOT + i]
        o_ref[i] = jnp.where(slot >= 0, p_ref[jnp.maximum(slot, 0)], 0.0)
        return carry

    lax.fori_loop(0, o_ref.shape[0], one, 0)


def unpack_kernel(tab, near_ref, got_ref, o_ref):
    sib, slab, cells = o_ref.shape
    blocks = cells // BLK
    at = pl.multiple_of(tab[HALF] * slab, SUB)
    for j in range(sib):
        for b in range(blocks):
            slot = tab[COL_SLOT + j * blocks + b]
            use = jnp.maximum(slot, 0)
            total = near_ref[use, pl.ds(at, slab), :] + got_ref[use]
            o_ref[j, :, b * BLK : (b + 1) * BLK] = jnp.where(slot >= 0, total, 0.0)


def listed_products(cap, sib, table, scattered, a_hi, a_lo):
    row_cells, col_cells = a_hi.shape
    pieces, blocks, sub, width = scattered.shape
    near_chunks = lax.axis_size("row_0")
    half_rows = width // (near_chunks * lax.axis_size("row_1"))
    own = pl.pallas_call(
        functools.partial(pick_kernel, cap),
        out_shape=jax.ShapeDtypeStruct((cap, sub, width), jnp.float32),
        in_specs=[SMEM, VMEM],
        out_specs=VMEM,
        compiler_params=pltpu.CompilerParams(vmem_limit_bytes=8 << 20),
    )(table, scattered.reshape(pieces * blocks, sub, width))
    right = turned(own, "col_x", 1)
    left = turned(own, "col_x", -1)
    beside = swapped(own, "col_y", 1)
    right_beside = turned(beside, "col_x", 1)
    left_beside = turned(beside, "col_x", -1)
    right_two = turned(right, "col_x", 1)
    left_two = turned(left_beside, "col_x", -1)
    g0 = jnp.stack([own, beside, right, left])
    g1 = jnp.stack([right_beside, left_beside, right_two, left_two])
    c0 = swapped(g0, "core", 1)
    c1 = swapped(g1, "core", 1)
    chunk = width // near_chunks
    u, p = pl.pallas_call(
        functools.partial(product_kernel, cap, sib),
        out_shape=(
            jax.ShapeDtypeStruct((near_chunks, cap, chunk, BLK), jnp.float32),
            jax.ShapeDtypeStruct((cap, BLK, width), jnp.float32),
        ),
        in_specs=[SMEM] + [VMEM] * 6,
        out_specs=(VMEM, VMEM),
        scratch_shapes=[
            pltpu.VMEM((row_cells // BLK // 2, width, 6 * BLK), jnp.bfloat16),
            pltpu.VMEM((width, 2 * BLK), jnp.float32),
        ],
        compiler_params=pltpu.CompilerParams(vmem_limit_bytes=40 << 20),
    )(table, g0, g1, c0, c1, a_hi, a_lo)
    near = lax.psum_scatter(u, "row_0", scatter_dimension=0, tiled=True)[0]
    panels = pl.pallas_call(
        spread_kernel,
        out_shape=jax.ShapeDtypeStruct((sib * row_cells // BLK, BLK, width), jnp.float32),
        in_specs=[SMEM, VMEM],
        out_specs=VMEM,
        compiler_params=pltpu.CompilerParams(vmem_limit_bytes=16 << 20),
        cost_estimate=pl.CostEstimate(flops=0, transcendentals=0, bytes_accessed=10 << 20),
    )(table, p)
    half = lax.axis_index("row_1")
    sent = lax.dynamic_slice_in_dim(near, (1 - half) * half_rows, half_rows, 1)
    got = swapped(sent, "row_1", 1)
    upper_part = pl.pallas_call(
        unpack_kernel,
        out_shape=jax.ShapeDtypeStruct((sib, half_rows, col_cells), jnp.float32),
        in_specs=[SMEM, VMEM, VMEM],
        out_specs=VMEM,
        compiler_params=pltpu.CompilerParams(vmem_limit_bytes=8 << 20),
    )(table, near, got)
    return upper_part, panels


def piece_columns():
    y = lax.axis_index("col_y")
    x = lax.axis_index("col_x")
    core = lax.axis_index("core")
    n_x = lax.axis_size("col_x")
    places = [(y, x), (1 - y, x), (y, x - 1), (y, x + 1)]
    places += [(1 - y, x - 1), (1 - y, x + 1), (y, x - 2), (1 - y, x + 2)]
    return jnp.stack(
        [
            (py * n_x + (px + n_x) % n_x) * 2 + pc
            for pc in (core, 1 - core)
            for py, px in places
        ]
    ).astype(jnp.int32)


def per_device(anc_inverse, l_store, diag_inv, block_lists, block_counts, sibling_columns):
    row_cells, col_cells = anc_inverse.shape
    width = l_store.shape[2]
    sib = sibling_columns.shape[0]
    n_col = lax.axis_size(COL)
    n_row = lax.axis_size(ROW)
    row_index = lax.axis_index(ROW)
    col_index = lax.axis_index(COL)
    blocks = row_cells // BLK
    cut = l_store[0].reshape(blocks, n_col, SUB, width).transpose(1, 0, 2, 3)
    scattered = lax.all_to_all(cut, COL, 0, 0, tiled=True)
    rounded = lax.reduce_precision(anc_inverse, 8, 7)
    a_hi = rounded.astype(jnp.bfloat16)
    a_lo = (anc_inverse - rounded).astype(jnp.bfloat16)

    listed = member_blocks(block_lists, block_counts, n_row * blocks)
    groups = listed.reshape(sib, n_row, blocks)
    most = jnp.max(jnp.sum(groups, axis=(0, 2)))
    row_code, row_start, row_slot = slot_tables(
        lax.dynamic_index_in_dim(groups, row_index, 1, keepdims=False)
    )
    col_code, col_start, col_slot = slot_tables(
        lax.dynamic_index_in_dim(groups, col_index, 1, keepdims=False)
    )
    owner = jnp.sum(
        jnp.where(
            (row_code // blocks)[:, None] == jnp.arange(sib, dtype=jnp.int32)[None, :],
            sibling_columns[None, :],
            0,
        ),
        axis=1,
    )
    table = jnp.concatenate(
        [
            padded(row_code % blocks, 64),
            padded(row_start, 8),
            padded(col_code % blocks, 64),
            padded(col_start, 8),
            padded(piece_columns(), 16),
            padded(row_slot, 64),
            padded(col_slot, 64),
            padded(owner * blocks + row_code % blocks, 64),
            padded(lax.axis_index("row_1")[None], 8),
        ]
    )
    caps = [c for c in CAPS if c < sib * blocks] + [sib * blocks]
    which = sum((most > c).astype(jnp.int32) for c in caps[:-1])
    upper_part, panels = lax.switch(
        which,
        [functools.partial(listed_products, c, sib) for c in caps],
        table,
        scattered,
        a_hi,
        a_lo,
    )
    by_width = lax.all_to_all(upper_part.transpose(1, 0, 2), COL, 0, 0, tiled=True)
    moved = lax.all_to_all(by_width, ROW, 0, 0, tiled=True)
    slots = jnp.zeros((n_col, n_row, col_cells), jnp.float32)
    for j in range(sib):
        slots = lax.dynamic_update_slice_in_dim(slots, moved[None, :, j], sibling_columns[j], 0)
    gathered = lax.all_to_all(slots, COL, 0, 0, tiled=True)
    inner = jnp.einsum(
        "rjt,jtv->jrv",
        moved,
        panels.reshape(sib, row_cells, width),
        precision=lax.Precision.HIGH,
        preferred_element_type=jnp.float32,
    )
    inner = inner + swapped(inner, "row_1", 1)
    for step in (1, 2, 4):
        inner = inner + swapped(inner, "row_0", step)
    gathered, inner = lax.optimization_barrier((gathered, inner))
    diag_slots = jnp.zeros((n_col, n_row, width), jnp.float32)
    for j in range(sib):
        diag_slots = lax.dynamic_update_slice_in_dim(
            diag_slots, inner[j][None], sibling_columns[j], 0
        )
    diag_parts = lax.all_to_all(diag_slots, COL, 0, 0, tiled=True)
    lower_out = gathered.transpose(2, 1, 0).reshape(1, row_cells, width)
    diag_total = diag_parts.transpose(1, 0, 2).reshape(width, width)
    present = jnp.sum((sibling_columns == col_index).astype(jnp.float32))
    diag_out = (present * diag_inv[0] - diag_total)[None]
    return (upper_part, lower_out, diag_out)


def solution(mesh):
    finer = Mesh(mesh.devices.reshape(8, 2, 2, 4, 2), ROW + COL)
    return jax.shard_map(
        per_device,
        mesh=finer,
        in_specs=(P(ROW, COL), P(COL, ROW, None), P(COL, None, None), P(), P(), P()),
        out_specs=(P(None, ROW, COL), P(COL, ROW, None), P(COL, None, None)),
        check_vma=False,
    )
```

time: 276 us -> 252 us (0.913)
  waiting for transfers between devices: 151 us -> 114 us
  starting transfers between devices: 28.7 us -> 50.4 us
  blocking collectives: 33 us -> 13.6 us
  Pallas kernels: 0 us -> 17.7 us
  matrix products: 19.2 us -> 3.91 us
  local copies, waits for them, and re-layouts: 13.1 us -> 21 us
    all_gather x1 -> x0, waiting for transfers between devices: 40.4 us -> none  [per_device(): panels = lax.all_gather(owned, 'col', axis=0, tiled=False)]
    all_to_all x2 -> x1, blocking collectives: 33 us -> 13.6 us  [per_device(): lax.all_to_all(upper_part.transpose(1, 0, 2), COL, 0, 0, tiled=True)]
    pallas_call x0 -> x4, Pallas kernels: none -> 17.7 us  [the longest x1 11.2 us: listed_products(): pl.pallas_call(functools.partial(product_kernel, cap, sib), out_shape=(ja...]
    dot_general x2 -> x1, matrix products: 19.2 us -> 3.91 us  [per_device(): jnp.einsum('rjt,jtv->jrv', moved, panels.reshape(sib, row_cells, width),...]
    all_to_all x3 -> x4, starting transfers between devices: 22.8 us -> 30.4 us  [the longest x1 10.1 us: per_device(): diag_parts = lax.all_to_all(diag_slots, COL, 0, 0, tiled=True)]
    ppermute x5 -> x8, starting transfers between devices: 5.84 us -> 13.4 us  [swapped(): return lax.ppermute(x, axis, [(i, i ^ bit) for i in range(length)])]
    reduce_scatter x1, waiting for transfers between devices: 65.3 us -> 57.9 us  [listed_products(): near = lax.psum_scatter(u, 'row_0', scatter_dimension=0, tiled=True)[0]]
    cond x0 -> x11, local copies, waits for them, and re-layouts: none -> 6.87 us
  transfers between devices with their start and end apart: 10 -> 19, of which waited for: 9 -> 13; matrix products, arithmetic and copies ran while one was open for 4% -> 6% of each run, Pallas kernels for 0% -> 2%
where the time goes in v3:
time: 252 us; the launch traced here: 253 us
  waiting for transfers between devices  114 us (45%)
  starting transfers between devices  50.4 us (20%)
  between operations  22.6 us (9%)
  local copies, waits for them, and re-layouts  21 us (8%)
  Pallas kernels  17.7 us (7%)
  blocking collectives  13.6 us (5%)
  other arithmetic  9.66 us (4%)
  matrix products  3.91 us (2%)
    reduce_scatter x1, waiting for transfers between devices, listed_products(): near = lax.psum_scatter(u, 'row_0', scatter_dimension=0, tiled=True)[0]  57.9 us
    ppermute x8, waiting for transfers between devices, swapped(): return lax.ppermute(x, axis, [(i, i ^ bit) for i in range(length)])  32.7 us
    all_to_all x1, blocking collectives, per_device(): lax.all_to_all(upper_part.transpose(1, 0, 2), COL, 0, 0, tiled=True)  13.6 us
    ppermute x8, starting transfers between devices, swapped(): return lax.ppermute(x, axis, [(i, i ^ bit) for i in range(length)])  13.4 us
    pallas_call x1, Pallas kernels, listed_products(): pl.pallas_call(functools.partial(product_kernel, cap, sib), out_shape=(ja...  11.2 us
    all_to_all x1, starting transfers between devices, per_device(): diag_parts = lax.all_to_all(diag_slots, COL, 0, 0, tiled=True)  10.1 us
    all_to_all x1, waiting for transfers between devices, per_device(): scattered = lax.all_to_all(cut, COL, 0, 0, tiled=True)  10 us
    all_to_all x1, starting transfers between devices, per_device(): scattered = lax.all_to_all(cut, COL, 0, 0, tiled=True)  7.49 us
  transfers between devices with their start and end apart: 19, of which 13 were waited for; matrix products, arithmetic and copies ran while one was open for 6% of the time, Pallas kernels for 2%

profile of v3, /device:TPU:1, one launch (start us, length us, event | category | flops | bytes accessed | tf_op | source)
XLA Modules:
  0.0 252.7 jit_solution(5661187546356967021)
XLA Ops:
  7.2 2.5 copy.41
  9.7 7.5 %all-to-all-start = ((f32[16,10,8,256]{3,2,1,0:T(8,128)}), f32[16,10,8,256]{3,2,1,0:T(8,128)}, u32[]{:S(2)}, u32[]{:S(2)}) async-start(f32[16,10,8,256]{3,2,1,0:T(8,128)} %copy.41), calls=%async_computation.2 | async-start | bytes 2621440 | tf_op jit(solution)/shard_map/all_to_all | solution.py:243
  17.3 0.2 fusion.4
  18.6 0.2 select_reduce_fusion.4
  18.9 0.1 reduce_sum.90
  19.0 0.6 reduce_max.9
  20.4 5.6 %fusion = (bf16[1280,1280]{1,0:T(8,128)(2,1)S(1)}, bf16[1280,1280]{1,0:T(8,128)(2,1)}) fusion(f32[1280,1280]{1,0:T(8,128)} %param.8), kind=kLoop, calls=%fused_computation.8 | loop fusion | flops 6553600 | bytes 13107200 | tf_op jit(solution)/shard_map/convert_element_type | solution.py:246
  26.0 10.0 %all-to-all-done = f32[16,10,8,256]{3,2,1,0:T(8,128)} async-done(((f32[16,10,8,256]{3,2,1,0:T(8,128)}), f32[16,10,8,256]{3,2,1,0:T(8,128)}, u32[]{:S(2)}, u32[]{:S(2)}) %all-to-all-start) | async-done | bytes 1310752 | tf_op jit(solution)/shard_map/all_to_all | solution.py:243
  36.0 111.8 %conditional.1 = (f32[4,16,1280]{2,1,0:T(8,128)}, f32[4,1280,256]{2,1,0:T(8,128)}) conditional(s32[]{:T(128)} %clamp.3, (f32[16,10,8,256]{3,2,1,0:T(8,128)}, s32[360]{0:T(512)S(1)}, bf16[1280,1280]{1,0:T(8,128)(2,1)}, bf16[1280,1280]{1,0:T(8,128)(2,1)S(1)}) %tuple.19, (f32[16,10,8,256]{3,2,1,0:T(8,128)}, s32[360]{0:T(512)S(1)}, ...), branch_computations={%region_11.13_spmd, %region_13.15_spmd} | conditional | flops 1966088 | bytes 112722584 | solution.py:280
  36.0 1.4 branch_0_fun.4
  37.4 0.3 collective-permute-start
  37.7 0.2 collective-permute-start.1
  37.9 6.0 %collective-permute-done = f32[28,8,256]{2,1,0:T(8,128)S(1)} collective-permute-done((f32[28,8,256]{2,1,0:T(8,128)S(1)}, f32[28,8,256]{2,1,0:T(8,128)S(1)}, u32[]{:S(2)}, u32[]{:S(2)}) %collective-permute-start) | collective-permute-done | bytes 229408 | tf_op jit(solution)/shard_map/cond/branch_0_fun/ppermute | solution.py:26
  43.9 1.4 collective-permute-start.4
  45.3 0.3 collective-permute-start.2
  45.6 1.2 collective-permute-start.3
  46.9 2.6 %collective-permute-done.4 = f32[28,8,256]{2,1,0:T(8,128)S(1)} collective-permute-done((f32[28,8,256]{2,1,0:T(8,128)S(1)}, f32[28,8,256]{2,1,0:T(8,128)S(1)}, u32[]{:S(2)}, u32[]{:S(2)}) %collective-permute-start.4) | collective-permute-done | bytes 229408 | tf_op jit(solution)/shard_map/cond/branch_0_fun/ppermute | solution.py:31
  49.4 3.4 %collective-permute-start.6 = (f32[28,8,256]{2,1,0:T(8,128)S(1)}, f32[28,8,256]{2,1,0:T(8,128)S(1)}, u32[]{:S(2)}, u32[]{:S(2)}) collective-permute-start(f32[28,8,256]{2,1,0:T(8,128)S(1)} %collective-permute-done.4), channel_id=1, source_target_pairs={{0,6},{2,0},{4,2},{6,4},{1,7},{3,1},{5,3},{7,5},{8,14},{10,8},{12,... | collective-permute-start | bytes 688136 | tf_op jit(solution)/shard_map/cond/branch_0_fun/ppermute | solution.py:31
  52.8 1.6 collective-permute-done.2
  54.4 4.7 %collective-permute-start.7 = (f32[4,28,8,256]{3,2,1,0:T(8,128)S(1)}, f32[4,28,8,256]{3,2,1,0:T(8,128)S(1)}, u32[]{:S(2)}, u32[]{:S(2)}) collective-permute-start(f32[4,28,8,256]{3,2,1,0:T(8,128)S(1)} %pad_maximum_fusion.g0), channel_id=1, source_target_pairs={{0,1},{1,0},{2,3},{3,2},{4,5},{5,4},{6,7},{7,6},{8,9},{9,8},{10,11... | collective-permute-start | bytes 2752520 | tf_op jit(solution)/shard_map/cond/branch_0_fun/ppermute | solution.py:26
  59.1 0.1 collective-permute-done.6
  59.3 2.6 %collective-permute-start.8 = (f32[4,28,8,256]{3,2,1,0:T(8,128)S(1)}, f32[4,28,8,256]{3,2,1,0:T(8,128)S(1)}, u32[]{:S(2)}, u32[]{:S(2)}) collective-permute-start(f32[4,28,8,256]{3,2,1,0:T(8,128)S(1)} %pad_maximum_fusion.1.g1), channel_id=1, source_target_pairs={{0,1},{1,0},{2,3},{3,2},{4,5},{5,4},{6,7},{7,6},{8,9},{9,8},{10,11... | collective-permute-start | bytes 2752520 | tf_op jit(solution)/shard_map/cond/branch_0_fun/ppermute | solution.py:26
  61.9 2.1 collective-permute-done.8.c1
  64.0 11.2 %branch_0_fun.5 = (f32[8,28,32,128]{3,2,1,0:T(8,128)S(1)}, f32[28,128,256]{2,1,0:T(8,128)S(1)}) custom-call(s32[360]{0:T(512)S(1)} %get-tuple-element.17.tab, f32[4,28,8,256]{3,2,1,0:T(8,128)S(1)} %pad_maximum_fusion.g0, f32[4,28,8,256]{3,2,1,0:T(8,128)S(1)} %pad_maximum_fusion.1.g1, f32[4,28,8,256]{3,2,1,0:T(8,128)S(1)} %collective-permute-done.7.c0, ...), custom_call_target="tpu_custom_call" | custom-call | tf_op jit(solution)/shard_map/cond/branch_0_fun/pallas_call | solution.py:181
  75.2 1.8 copy-done.2
  77.0 1.8 copy-done.4
  78.9 57.9 %reduce-scatter.3.cloned.1.call-done = f32[1,28,32,128]{3,2,1,0:T(8,128)} async-done(((f32[8,28,32,128]{3,2,1,0:T(8,128)}), f32[1,28,32,128]{3,2,1,0:T(8,128)}) %reduce-scatter.3.cloned.1.call-update) | async-done | bytes 458768 | tf_op jit(solution)/shard_map/cond/branch_0_fun/reduce_scatter | solution.py:195
  136.8 1.0 dynamic-slice_bitcast_fusion
  137.8 2.8 %collective-permute-start.9 = (f32[28,16,128]{2,1,0:T(8,128)S(1)}, f32[28,16,128]{2,1,0:T(8,128)S(1)}, u32[]{:S(2)}, u32[]{:S(2)}) collective-permute-start(f32[28,16,128]{2,1,0:T(8,128)S(1)} %dynamic-slice_bitcast_fusion), channel_id=1, source_target_pairs={{0,16},{16,0},{1,17},{17,1},{2,18},{18,2},{3,19},{19,3},{4,20},{20... | collective-permute-start | bytes 688136 | tf_op jit(solution)/shard_map/cond/branch_0_fun/ppermute | solution.py:26
  140.6 2.0 copy-done.3
  142.6 3.8 %branch_0_fun.7 = f32[40,128,256]{2,1,0:T(8,128)} custom-call(s32[360]{0:T(512)S(1)} %get-tuple-element.17.tab, f32[28,128,256]{2,1,0:T(8,128)S(1)} %copy-done.3), custom_call_target="tpu_custom_call" | custom-call | bytes 10485760 | tf_op jit(solution)/shard_map/cond/branch_0_fun/pallas_call | solution.py:196
  146.4 1.4 branch_0_fun.6
  147.8 1.2 copy.58
  149.0 13.6 %all_to_all.25 = f32[16,4,1280]{2,1,0:T(4,128)} all-to-all(f32[16,4,1280]{2,1,0:T(4,128)S(1)} %bitcast.75), channel_id=1, replica_groups=mesh['row_0'=8,'row_1'=2,'col_y'=2,'col_x'=4,'core'=2] {'col_y','col_x',..., dimensions={0} | all-to-all | bytes 655360 | tf_op jit(solution)/shard_map/all_to_all | solution.py:288
  162.7 6.4 %all-to-all-start.2 = ((f32[16,4,1280]{2,1,0:T(4,128)}), f32[16,4,1280]{2,1,0:T(4,128)S(1)}, u32[]{:S(2)}, u32[]{:S(2)}) async-start(f32[16,4,1280]{2,1,0:T(4,128)} %all_to_all.25), calls=%async_computation.4 | async-start | bytes 655360 | tf_op jit(solution)/shard_map/all_to_all | solution.py:289
  169.1 0.7 fusion.10
  177.5 4.4 %all-to-all-done.2 = f32[16,4,1280]{2,1,0:T(4,128)S(1)} async-done(((f32[16,4,1280]{2,1,0:T(4,128)}), f32[16,4,1280]{2,1,0:T(4,128)S(1)}, u32[]{:S(2)}, u32[]{:S(2)}) %all-to-all-start.2) | async-done | bytes 327712 | tf_op jit(solution)/shard_map/all_to_all | solution.py:289
  181.9 0.2 slice_bitcast_fusion
  182.1 1.2 broadcast_in_dim.109
  183.3 0.6 copy_dynamic-update-slice_fusion.3
  183.9 0.6 copy_dynamic-update-slice_fusion.2
  184.6 0.6 copy_dynamic-update-slice_fusion.1
  185.2 0.6 copy_dynamic-update-slice_fusion
  185.9 6.5 %all-to-all-start.3 = ((f32[16,16,1280]{2,1,0:T(8,128)}), f32[16,16,1280]{2,1,0:T(8,128)S(1)}, u32[]{:S(2)}, u32[]{:S(2)}) async-start(f32[16,16,1280]{2,1,0:T(8,128)} %copy_dynamic-update-slice_fusion), calls=%async_computation.5 | async-start | bytes 2621440 | tf_op jit(solution)/shard_map/all_to_all | solution.py:293
  192.3 3.9 %fusion.1 = f32[4,16,256]{2,1,0:T(8,128)S(1)} fusion(f32[4,1280,256]{2,1,0:T(8,128)} %get-tuple-element.37, f32[16,4,1280]{2,1,0:T(4,128)S(1)} %all-to-all-done.2), kind=kOutput, calls=%fused_computation.9 | convolution fusion | flops 125829120 | bytes 5636096 | tf_op jit(solution)/shard_map/rjt,jtv->jrv/dot_general | solution.py:294
  196.2 0.4 collective-permute-start.20
  196.6 11.3 %collective-permute-done.20 = f32[4,16,256]{2,1,0:T(8,128)S(1)} collective-permute-done((f32[4,16,256]{2,1,0:T(8,128)S(1)}, f32[4,16,256]{2,1,0:T(8,128)S(1)}, u32[]{:S(2)}, u32[]{:S(2)}) %collective-permute-start.20) | collective-permute-done | bytes 65568 | tf_op jit(solution)/shard_map/ppermute | solution.py:26
  208.1 3.3 %collective-permute-done.21 = f32[4,16,256]{2,1,0:T(8,128)S(1)} collective-permute-done((f32[4,16,256]{2,1,0:T(8,128)S(1)}, f32[4,16,256]{2,1,0:T(8,128)S(1)}, u32[]{:S(2)}, u32[]{:S(2)}) %collective-permute-start.21) | collective-permute-done | bytes 65568 | tf_op jit(solution)/shard_map/ppermute | solution.py:26
  211.4 0.7 collective-permute-start.22
  212.2 3.9 %collective-permute-done.22 = f32[4,16,256]{2,1,0:T(8,128)S(1)} collective-permute-done((f32[4,16,256]{2,1,0:T(8,128)S(1)}, f32[4,16,256]{2,1,0:T(8,128)S(1)}, u32[]{:S(2)}, u32[]{:S(2)}) %collective-permute-start.22) | collective-permute-done | bytes 65568 | tf_op jit(solution)/shard_map/ppermute | solution.py:26
  216.0 1.8 collective-permute-start.23
  217.8 6.1 %collective-permute-done.23 = f32[4,16,256]{2,1,0:T(8,128)S(1)} collective-permute-done((f32[4,16,256]{2,1,0:T(8,128)S(1)}, f32[4,16,256]{2,1,0:T(8,128)S(1)}, u32[]{:S(2)}, u32[]{:S(2)}) %collective-permute-start.23) | collective-permute-done | bytes 65568 | tf_op jit(solution)/shard_map/ppermute | solution.py:26
  223.9 0.7 broadcast_in_dim.110
  224.6 0.6 slice_dynamic-update-slice_fusion.3
  225.2 0.6 slice_dynamic-update-slice_fusion.2
  225.8 0.6 slice_dynamic-update-slice_fusion.1
  226.4 0.6 slice_dynamic-update-slice_fusion
  227.0 10.1 %all-to-all-start.4 = ((f32[16,16,256]{2,1,0:T(8,128)}), f32[16,16,256]{2,1,0:T(8,128)S(1)}, u32[]{:S(2)}, u32[]{:S(2)}) async-start(f32[16,16,256]{2,1,0:T(8,128)} %slice_dynamic-update-slice_fusion), calls=%async_computation.6 | async-start | bytes 524288 | tf_op jit(solution)/shard_map/all_to_all | solution.py:310
  237.1 0.7 fusion.9
  237.8 0.8 copy.48
  238.5 1.5 copy.50
  240.0 4.3 %all-to-all-done.4 = f32[16,16,256]{2,1,0:T(8,128)S(1)} async-done(((f32[16,16,256]{2,1,0:T(8,128)}), f32[16,16,256]{2,1,0:T(8,128)S(1)}, u32[]{:S(2)}, u32[]{:S(2)}) %all-to-all-start.4) | async-done | bytes 262176 | tf_op jit(solution)/shard_map/all_to_all | solution.py:310
  244.3 0.2 copy.49
  244.5 1.4 bitcast_subtract_fusion
  (59 shorter events, 1.6 us)
Async XLA Ops:
  9.7 7.5 %copy-start.12 = (s32[4]{0:T(128)S(1)}, s32[4]{0:T(128)}, u32[]{:S(2)}) copy-start(s32[4]{0:T(128)} %param.12) | copy-start | bytes 52
  9.7 7.6 %copy-start.11 = (s32[4,96]{1,0:T(4,128)S(1)}, s32[4,96]{1,0:T(4,128)}, u32[]{:S(2)}) copy-start(s32[4,96]{1,0:T(4,128)} %param.11) | copy-start | bytes 4612
  9.7 8.7 %copy-start.10 = (s32[4]{0:T(128)S(1)}, s32[4]{0:T(128)}, u32[]{:S(2)}) copy-start(s32[4]{0:T(128)} %param.13) | copy-start | bytes 52
  9.7 26.4 %all-to-all-start = ((f32[16,10,8,256]{3,2,1,0:T(8,128)}), f32[16,10,8,256]{3,2,1,0:T(8,128)}, u32[]{:S(2)}, u32[]{:S(2)}) async-start(f32[16,10,8,256]{3,2,1,0:T(8,128)} %copy.41), calls=%async_computation.2 | async-start | bytes 2621440 | tf_op jit(solution)/shard_map/all_to_all | solution.py:243
  36.0 100.8 %reduce-scatter.3.cloned.1.call-start = ((), (), s32[]{:S(2)}) async-start(), calls=%async_computation.7 | async-start | bytes 4128768 | tf_op jit(solution)/shard_map/cond/branch_0_fun/reduce_scatter | solution.py:195
  37.4 6.5 %collective-permute-start = (f32[28,8,256]{2,1,0:T(8,128)S(1)}, f32[28,8,256]{2,1,0:T(8,128)S(1)}, u32[]{:S(2)}, u32[]{:S(2)}) collective-permute-start(f32[28,8,256]{2,1,0:T(8,128)S(1)} %branch_0_fun.4), channel_id=1, source_target_pairs={{0,8},{8,0},{1,9},{9,1},{2,10},{10,2},{3,11},{11,3},{4,12},{12,4},... | collective-permute-start | bytes 688136 | tf_op jit(solution)/shard_map/cond/branch_0_fun/ppermute | solution.py:26
  37.7 9.1 %collective-permute-start.1 = (f32[28,8,256]{2,1,0:T(8,128)S(1)}, f32[28,8,256]{2,1,0:T(8,128)S(1)}, u32[]{:S(2)}, u32[]{:S(2)}) collective-permute-start(f32[28,8,256]{2,1,0:T(8,128)S(1)} %branch_0_fun.4), channel_id=1, source_target_pairs={{0,2},{2,4},{4,6},{6,0},{1,3},{3,5},{5,7},{7,1},{8,10},{10,12},{12... | collective-permute-start | bytes 688136 | tf_op jit(solution)/shard_map/cond/branch_0_fun/ppermute | solution.py:31
  43.9 5.5 %collective-permute-start.4 = (f32[28,8,256]{2,1,0:T(8,128)S(1)}, f32[28,8,256]{2,1,0:T(8,128)S(1)}, u32[]{:S(2)}, u32[]{:S(2)}) collective-permute-start(f32[28,8,256]{2,1,0:T(8,128)S(1)} %collective-permute-done), channel_id=1, source_target_pairs={{0,6},{2,0},{4,2},{6,4},{1,7},{3,1},{5,3},{7,5},{8,14},{10,8},{12,... | collective-permute-start | bytes 688136 | tf_op jit(solution)/shard_map/cond/branch_0_fun/ppermute | solution.py:31
  45.3 9.0 %collective-permute-start.2 = (f32[28,8,256]{2,1,0:T(8,128)S(1)}, f32[28,8,256]{2,1,0:T(8,128)S(1)}, u32[]{:S(2)}, u32[]{:S(2)}) collective-permute-start(f32[28,8,256]{2,1,0:T(8,128)S(1)} %branch_0_fun.4), channel_id=1, source_target_pairs={{0,6},{2,0},{4,2},{6,4},{1,7},{3,1},{5,3},{7,5},{8,14},{10,8},{12,... | collective-permute-start | bytes 688136 | tf_op jit(solution)/shard_map/cond/branch_0_fun/ppermute | solution.py:31
  45.6 13.5 %collective-permute-start.3 = (f32[28,8,256]{2,1,0:T(8,128)S(1)}, f32[28,8,256]{2,1,0:T(8,128)S(1)}, u32[]{:S(2)}, u32[]{:S(2)}) collective-permute-start(f32[28,8,256]{2,1,0:T(8,128)S(1)} %collective-permute-done), channel_id=1, source_target_pairs={{0,2},{2,4},{4,6},{6,0},{1,3},{3,5},{5,7},{7,1},{8,10},{10,12},{12... | collective-permute-start | bytes 688136 | tf_op jit(solution)/shard_map/cond/branch_0_fun/ppermute | solution.py:31
  46.8 12.3 %collective-permute-start.5 = (f32[28,8,256]{2,1,0:T(8,128)S(1)}, f32[28,8,256]{2,1,0:T(8,128)S(1)}, u32[]{:S(2)}, u32[]{:S(2)}) collective-permute-start(f32[28,8,256]{2,1,0:T(8,128)S(1)} %collective-permute-done.1), channel_id=1, source_target_pairs={{0,2},{2,4},{4,6},{6,0},{1,3},{3,5},{5,7},{7,1},{8,10},{10,12},{12... | collective-permute-start | bytes 688136 | tf_op jit(solution)/shard_map/cond/branch_0_fun/ppermute | solution.py:31
  49.4 9.8 %collective-permute-start.6 = (f32[28,8,256]{2,1,0:T(8,128)S(1)}, f32[28,8,256]{2,1,0:T(8,128)S(1)}, u32[]{:S(2)}, u32[]{:S(2)}) collective-permute-start(f32[28,8,256]{2,1,0:T(8,128)S(1)} %collective-permute-done.4), channel_id=1, source_target_pairs={{0,6},{2,0},{4,2},{6,4},{1,7},{3,1},{5,3},{7,5},{8,14},{10,8},{12,... | collective-permute-start | bytes 688136 | tf_op jit(solution)/shard_map/cond/branch_0_fun/ppermute | solution.py:31
  54.3 9.7 %copy-start.7 = (bf16[1280,1280]{1,0:T(8,128)(2,1)S(1)}, bf16[1280,1280]{1,0:T(8,128)(2,1)}, u32[]{:S(2)}) copy-start(bf16[1280,1280]{1,0:T(8,128)(2,1)} %get-tuple-element.19.ah) | copy-start | bytes 9830404 | tf_op jit(solution)/shard_map/cond
  54.4 7.5 %collective-permute-start.7 = (f32[4,28,8,256]{3,2,1,0:T(8,128)S(1)}, f32[4,28,8,256]{3,2,1,0:T(8,128)S(1)}, u32[]{:S(2)}, u32[]{:S(2)}) collective-permute-start(f32[4,28,8,256]{3,2,1,0:T(8,128)S(1)} %pad_maximum_fusion.g0), channel_id=1, source_target_pairs={{0,1},{1,0},{2,3},{3,2},{4,5},{5,4},{6,7},{7,6},{8,9},{9,8},{10,11... | collective-permute-start | bytes 2752520 | tf_op jit(solution)/shard_map/cond/branch_0_fun/ppermute | solution.py:26
  59.3 4.7 %collective-permute-start.8 = (f32[4,28,8,256]{3,2,1,0:T(8,128)S(1)}, f32[4,28,8,256]{3,2,1,0:T(8,128)S(1)}, u32[]{:S(2)}, u32[]{:S(2)}) collective-permute-start(f32[4,28,8,256]{3,2,1,0:T(8,128)S(1)} %pad_maximum_fusion.1.g1), channel_id=1, source_target_pairs={{0,1},{1,0},{2,3},{3,2},{4,5},{5,4},{6,7},{7,6},{8,9},{9,8},{10,11... | collective-permute-start | bytes 2752520 | tf_op jit(solution)/shard_map/cond/branch_0_fun/ppermute | solution.py:26
  75.2 1.8 copy-start.2
  77.0 1.8 copy-start.4
  137.8 8.7 %collective-permute-start.9 = (f32[28,16,128]{2,1,0:T(8,128)S(1)}, f32[28,16,128]{2,1,0:T(8,128)S(1)}, u32[]{:S(2)}, u32[]{:S(2)}) collective-permute-start(f32[28,16,128]{2,1,0:T(8,128)S(1)} %dynamic-slice_bitcast_fusion), channel_id=1, source_target_pairs={{0,16},{16,0},{1,17},{17,1},{2,18},{18,2},{3,19},{19,3},{4,20},{20... | collective-permute-start | bytes 688136 | tf_op jit(solution)/shard_map/cond/branch_0_fun/ppermute | solution.py:26
  140.6 2.0 copy-start.3
  142.6 3.8 %copy-start.6 = (f32[1,28,32,128]{3,2,1,0:T(8,128)S(1)}, f32[1,28,32,128]{3,2,1,0:T(8,128)}, u32[]{:S(2)}) copy-start(f32[1,28,32,128]{3,2,1,0:T(8,128)} %reduce-scatter.3.cloned.1.call-done) | copy-start | bytes 1376260 | tf_op jit(solution)/shard_map/cond
  162.7 19.2 %all-to-all-start.2 = ((f32[16,4,1280]{2,1,0:T(4,128)}), f32[16,4,1280]{2,1,0:T(4,128)S(1)}, u32[]{:S(2)}, u32[]{:S(2)}) async-start(f32[16,4,1280]{2,1,0:T(4,128)} %all_to_all.25), calls=%async_computation.4 | async-start | bytes 655360 | tf_op jit(solution)/shard_map/all_to_all | solution.py:289
  185.9 38.0 %all-to-all-start.3 = ((f32[16,16,1280]{2,1,0:T(8,128)}), f32[16,16,1280]{2,1,0:T(8,128)S(1)}, u32[]{:S(2)}, u32[]{:S(2)}) async-start(f32[16,16,1280]{2,1,0:T(8,128)} %copy_dynamic-update-slice_fusion), calls=%async_computation.5 | async-start | bytes 2621440 | tf_op jit(solution)/shard_map/all_to_all | solution.py:293
  196.2 11.7 %collective-permute-start.20 = (f32[4,16,256]{2,1,0:T(8,128)S(1)}, f32[4,16,256]{2,1,0:T(8,128)S(1)}, u32[]{:S(2)}, u32[]{:S(2)}) collective-permute-start(f32[4,16,256]{2,1,0:T(8,128)S(1)} %fusion.1), channel_id=1, source_target_pairs={{0,16},{16,0},{1,17},{17,1},{2,18},{18,2},{3,19},{19,3},{4,20},{20... | collective-permute-start | bytes 196616 | tf_op jit(solution)/shard_map/ppermute | solution.py:26
  208.0 3.4 %collective-permute-start.21 = (f32[4,16,256]{2,1,0:T(8,128)S(1)}, f32[4,16,256]{2,1,0:T(8,128)S(1)}, u32[]{:S(2)}, u32[]{:S(2)}) collective-permute-start(f32[4,16,256]{2,1,0:T(8,128)S(1)} %add.282), channel_id=1, source_target_pairs={{0,32},{32,0},{64,96},{96,64},{128,160},{160,128},{192,224},{224,1... | collective-permute-start | bytes 196616 | tf_op jit(solution)/shard_map/ppermute | solution.py:26
  211.4 4.6 %collective-permute-start.22 = (f32[4,16,256]{2,1,0:T(8,128)S(1)}, f32[4,16,256]{2,1,0:T(8,128)S(1)}, u32[]{:S(2)}, u32[]{:S(2)}) collective-permute-start(f32[4,16,256]{2,1,0:T(8,128)S(1)} %add.283), channel_id=1, source_target_pairs={{0,64},{32,96},{64,0},{96,32},{128,192},{160,224},{192,128},{224,1... | collective-permute-start | bytes 196616 | tf_op jit(solution)/shard_map/ppermute | solution.py:26
  216.0 7.8 %collective-permute-start.23 = (f32[4,16,256]{2,1,0:T(8,128)S(1)}, f32[4,16,256]{2,1,0:T(8,128)S(1)}, u32[]{:S(2)}, u32[]{:S(2)}) collective-permute-start(f32[4,16,256]{2,1,0:T(8,128)S(1)} %add.284), channel_id=1, source_target_pairs={{0,128},{32,160},{64,192},{96,224},{128,0},{160,32},{192,64},{224,... | collective-permute-start | bytes 196616 | tf_op jit(solution)/shard_map/ppermute | solution.py:26
  227.0 17.2 %all-to-all-start.4 = ((f32[16,16,256]{2,1,0:T(8,128)}), f32[16,16,256]{2,1,0:T(8,128)S(1)}, u32[]{:S(2)}, u32[]{:S(2)}) async-start(f32[16,16,256]{2,1,0:T(8,128)} %slice_dynamic-update-slice_fusion), calls=%async_computation.6 | async-start | bytes 524288 | tf_op jit(solution)/shard_map/all_to_all | solution.py:310
  238.5 5.9 %copy-start.9 = (f32[1,256,256]{2,1,0:T(8,128)S(1)}, f32[1,256,256]{2,1,0:T(8,128)}, u32[]{:S(2)}) copy-start(f32[1,256,256]{2,1,0:T(8,128)} %param.10) | copy-start | bytes 786436
Sparse Core Ops, SparseCore 0:
  79.0 57.7 reduce-scatter.2

commit v4 on v3

--- a/solution.py
+++ b/solution.py
@@ -15,7 +15,7 @@
 CAPS = (28,)
 
 ROW_BLOCK, ROW_START, COL_BLOCK, COL_START = 0, 64, 72, 136
-PIECE, ROW_SLOT, COL_SLOT, SOURCE, HALF, TABLE = 144, 160, 224, 288, 352, 360
+PIECE, ROW_SLOT, COL_SLOT, SOURCE, OWNER, PRESENT, AT_ROW = 144, 160, 224, 288, 352, 360, 361
 
 SMEM = pl.BlockSpec(memory_space=pltpu.SMEM)
 VMEM = pl.BlockSpec(memory_space=pltpu.VMEM)
@@ -56,8 +56,11 @@
 
 
 def pick_kernel(cap, tab, x_ref, o_ref):
-    for q in range(cap):
+    def one(q, carry):
         o_ref[q] = x_ref[tab[SOURCE + q]]
+        return carry
+
+    lax.fori_loop(0, cap, one, 0)
 
 
 def product_kernel(cap, sib, tab, g0, g1, c0, c1, ah, al, u_ref, p_ref, lhs, acc):
@@ -77,14 +80,14 @@
         low = jnp.concatenate([tile(ref, b1, t0), tile(ref, b1, t1)], axis=1)
         return jnp.concatenate([top, low], axis=0)
 
-    for j in range(sib):
+    def sibling(j, outer):
         r0 = tab[ROW_START + j]
         r1 = tab[ROW_START + j + 1]
         n0 = tab[COL_START + j]
         n1 = tab[COL_START + j + 1]
         pairs = (r1 - r0 + 1) // 2
 
-        def split(i, carry, r0=r0, r1=r1):
+        def split(i, carry):
             q = r0 + 2 * i
             second = jnp.where(q + 1 < r1, p_ref[jnp.minimum(q + 1, cap - 1)], 0.0)
             block = jnp.concatenate([p_ref[q], second], axis=0).T
@@ -95,7 +98,7 @@
 
         lax.fori_loop(0, pairs, split, 0)
 
-        def columns(o, carry, r0=r0, n0=n0, n1=n1, pairs=pairs):
+        def columns(o, carry):
             s = n0 + 2 * o
             t0 = tab[COL_BLOCK + s]
             t1 = tab[COL_BLOCK + s + 1]
@@ -125,6 +128,9 @@
             return carry
 
         lax.fori_loop(0, (n1 - n0 + 1) // 2, columns, 0)
+        return outer
+
+    lax.fori_loop(0, sib, sibling, 0)
 
     def clear(s, carry):
         u_ref[:, s] = jnp.zeros((chunks, rows, BLK), jnp.float32)
@@ -133,25 +139,79 @@
     lax.fori_loop(tab[COL_START + sib], cap, clear, 0)
 
 
-def spread_kernel(tab, p_ref, o_ref):
-    def one(i, carry):
-        slot = tab[ROW_SLOT + i]
-        o_ref[i] = jnp.where(slot >= 0, p_ref[jnp.maximum(slot, 0)], 0.0)
+def unpack_kernel(base, tab, x_ref, o_ref):
+    sib, _, cells = o_ref.shape
+    blocks = cells // BLK
+
+    def sibling(j, carry):
+        for b in range(blocks):
+            slot = tab[base + j * blocks + b]
+            o_ref[j, :, b * BLK : (b + 1) * BLK] = jnp.where(
+                slot >= 0, x_ref[jnp.maximum(slot, 0)], 0.0
+            )
         return carry
 
-    lax.fori_loop(0, o_ref.shape[0], one, 0)
-
-
-def unpack_kernel(tab, near_ref, got_ref, o_ref):
-    sib, slab, cells = o_ref.shape
-    blocks = cells // BLK
-    at = pl.multiple_of(tab[HALF] * slab, SUB)
+    lax.fori_loop(0, sib, sibling, 0)
+
+
+def inner_kernel(sib, tab, x_ref, hi_ref, lo_ref, o_ref):
+    def sibling(j, carry):
+        def one(q, total):
+            x = x_ref[q]
+            x_hi = x.astype(jnp.bfloat16)
+            x_lo = (x - x_hi.astype(jnp.float32)).astype(jnp.bfloat16)
+            hi = hi_ref[q]
+            return total + jnp.dot(
+                jnp.concatenate([x_hi, x_lo, x_hi], axis=1),
+                jnp.concatenate([hi, hi, lo_ref[q]], axis=0),
+                preferred_element_type=jnp.float32,
+            )
+
+        o_ref[j] = lax.fori_loop(
+            tab[ROW_START + j],
+            tab[ROW_START + j + 1],
+            one,
+            jnp.zeros(o_ref.shape[1:], jnp.float32),
+        )
+        return carry
+
+    lax.fori_loop(0, sib, sibling, 0)
+
+
+def slots_kernel(tab, x_ref, inner_ref, o_ref):
+    sib, _, cells = x_ref.shape
+
+    def clear(d, carry):
+        o_ref[d] = jnp.zeros(o_ref.shape[1:], jnp.float32)
+        return carry
+
+    lax.fori_loop(0, o_ref.shape[0], clear, 0)
     for j in range(sib):
-        for b in range(blocks):
-            slot = tab[COL_SLOT + j * blocks + b]
-            use = jnp.maximum(slot, 0)
-            total = near_ref[use, pl.ds(at, slab), :] + got_ref[use]
-            o_ref[j, :, b * BLK : (b + 1) * BLK] = jnp.where(slot >= 0, total, 0.0)
+        at = tab[OWNER + j]
+        o_ref[at, :, :cells] = x_ref[j]
+        o_ref[at, :, cells:] = inner_ref[j]
+
+
+def finish_kernel(tab, x_ref, diag_ref, lower_ref, out_ref):
+    n_row = x_ref.shape[0]
+    cells = lower_ref.shape[0]
+    places = [lax.rem(2 * n_row - r - tab[AT_ROW], n_row) for r in range(n_row)]
+    for b in range(cells // BLK):
+        stack = jnp.concatenate([x_ref[p, :, b * BLK : (b + 1) * BLK] for p in places], axis=0)
+        lower_ref[b * BLK : (b + 1) * BLK, :] = stack.T
+    total = jnp.concatenate([x_ref[p, :, cells:] for p in places], axis=0)
+    out_ref[...] = jnp.where(tab[PRESENT] > 0, diag_ref[...] - total, 0.0)
+
+
+def ring_term(u, z, first, last):
+    part = lax.dynamic_index_in_dim(u, (z + 2 * u.shape[0]) % u.shape[0], 0, keepdims=False)
+    return part[first:last]
+
+
+def halves(up, down, half, rows):
+    return jnp.concatenate(
+        [lax.dynamic_slice_in_dim(x, half * rows, rows, 1) for x in (up, down)]
+    )
 
 
 def listed_products(cap, sib, table, scattered, a_hi, a_lo):
@@ -166,17 +226,27 @@
         out_specs=VMEM,
         compiler_params=pltpu.CompilerParams(vmem_limit_bytes=8 << 20),
     )(table, scattered.reshape(pieces * blocks, sub, width))
-    right = turned(own, "col_x", 1)
-    left = turned(own, "col_x", -1)
-    beside = swapped(own, "col_y", 1)
-    right_beside = turned(beside, "col_x", 1)
-    left_beside = turned(beside, "col_x", -1)
-    right_two = turned(right, "col_x", 1)
-    left_two = turned(left_beside, "col_x", -1)
-    g0 = jnp.stack([own, beside, right, left])
-    g1 = jnp.stack([right_beside, left_beside, right_two, left_two])
-    c0 = swapped(g0, "core", 1)
-    c1 = swapped(g1, "core", 1)
+    if cap < sib * blocks:
+        right = turned(own, "col_x", 1)
+        left = turned(own, "col_x", -1)
+        beside = swapped(own, "col_y", 1)
+        right_beside = turned(beside, "col_x", 1)
+        left_beside = turned(beside, "col_x", -1)
+        right_two = turned(right, "col_x", 1)
+        left_two = turned(left_beside, "col_x", -1)
+        g0 = jnp.stack([own, beside, right, left])
+        g1 = jnp.stack([right_beside, left_beside, right_two, left_two])
+        c0 = swapped(g0, "core", 1)
+        c1 = swapped(g1, "core", 1)
+    else:
+        all_pieces = lax.all_to_all(
+            jnp.broadcast_to(own[None], (pieces, *own.shape)), COL, 0, 0, tiled=True
+        )
+        order = piece_columns()
+        parts = jnp.concatenate(
+            [lax.dynamic_index_in_dim(all_pieces, order[i], 0) for i in range(pieces)]
+        )
+        g0, g1, c0, c1 = (parts[i : i + 4] for i in range(0, pieces, 4))
     chunk = width // near_chunks
     u, p = pl.pallas_call(
         functools.partial(product_kernel, cap, sib),
@@ -192,26 +262,45 @@
         ],
         compiler_params=pltpu.CompilerParams(vmem_limit_bytes=40 << 20),
     )(table, g0, g1, c0, c1, a_hi, a_lo)
-    near = lax.psum_scatter(u, "row_0", scatter_dimension=0, tiled=True)[0]
-    panels = pl.pallas_call(
-        spread_kernel,
-        out_shape=jax.ShapeDtypeStruct((sib * row_cells // BLK, BLK, width), jnp.float32),
+    z = lax.axis_index("row_0")
+    top = cap // 2
+    if cap < sib * blocks:
+        up = ring_term(u, z - 1, 0, top)
+        down = ring_term(u, z + 1, top, cap)
+        for step in range(1, near_chunks):
+            up = turned(up, "row_0", 1) + ring_term(u, z - 1 - step, 0, top)
+            down = turned(down, "row_0", -1) + ring_term(u, z + 1 + step, top, cap)
+    else:
+        near = jnp.sum(lax.all_to_all(u, "row_0", 0, 0, tiled=True), axis=0)
+        up, down = near[:top], near[top:]
+    half = lax.axis_index("row_1")
+    sent = halves(up, down, 1 - half, half_rows)
+    total = halves(up, down, half, half_rows) + swapped(sent, "row_1", 1)
+    unpack = lambda base, x: pl.pallas_call(
+        functools.partial(unpack_kernel, base),
+        out_shape=jax.ShapeDtypeStruct((sib, half_rows, col_cells), jnp.float32),
         in_specs=[SMEM, VMEM],
         out_specs=VMEM,
-        compiler_params=pltpu.CompilerParams(vmem_limit_bytes=16 << 20),
-        cost_estimate=pl.CostEstimate(flops=0, transcendentals=0, bytes_accessed=10 << 20),
-    )(table, p)
-    half = lax.axis_index("row_1")
-    sent = lax.dynamic_slice_in_dim(near, (1 - half) * half_rows, half_rows, 1)
-    got = swapped(sent, "row_1", 1)
-    upper_part = pl.pallas_call(
-        unpack_kernel,
-        out_shape=jax.ShapeDtypeStruct((sib, half_rows, col_cells), jnp.float32),
-        in_specs=[SMEM, VMEM, VMEM],
+        compiler_params=pltpu.CompilerParams(vmem_limit_bytes=8 << 20),
+        cost_estimate=pl.CostEstimate(flops=0, transcendentals=0, bytes_accessed=1 << 20),
+    )(table, x)
+    upper_part = unpack(COL_SLOT, total)
+    n_row = lax.axis_size(ROW)
+    n_col = lax.axis_size(COL)
+    spots = [(r, c) for r in range(n_row) for c in range(n_col)]
+    across = [(r * n_col + c, r * n_col + (-r - c) % n_col) for r, c in spots]
+    along = [(r * n_col + k, (-r - k) % n_row * n_col + k) for r, k in spots]
+    moved = lax.ppermute(lax.ppermute(total, ROW + COL, across), ROW + COL, along)
+    p_hi = lax.reduce_precision(p, 8, 7)
+    p_lo = (p - p_hi).astype(jnp.bfloat16)
+    inner = pl.pallas_call(
+        functools.partial(inner_kernel, sib),
+        out_shape=jax.ShapeDtypeStruct((sib, half_rows, width), jnp.float32),
+        in_specs=[SMEM] + [VMEM] * 3,
         out_specs=VMEM,
-        compiler_params=pltpu.CompilerParams(vmem_limit_bytes=8 << 20),
-    )(table, near, got)
-    return upper_part, panels
+        compiler_params=pltpu.CompilerParams(vmem_limit_bytes=12 << 20),
+    )(table, moved, p_hi.astype(jnp.bfloat16), p_lo)
+    return upper_part, unpack(ROW_SLOT, moved), inner
 
 
 def piece_columns():
@@ -272,12 +361,13 @@
             padded(row_slot, 64),
             padded(col_slot, 64),
             padded(owner * blocks + row_code % blocks, 64),
-            padded(lax.axis_index("row_1")[None], 8),
+            padded(sibling_columns, 8),
+            jnp.stack([jnp.any(sibling_columns == col_index).astype(jnp.int32), row_index]),
         ]
     )
     caps = [c for c in CAPS if c < sib * blocks] + [sib * blocks]
     which = sum((most > c).astype(jnp.int32) for c in caps[:-1])
-    upper_part, panels = lax.switch(
+    upper_part, moved, inner = lax.switch(
         which,
         [functools.partial(listed_products, c, sib) for c in caps],
         table,
@@ -285,34 +375,34 @@
         a_hi,
         a_lo,
     )
-    by_width = lax.all_to_all(upper_part.transpose(1, 0, 2), COL, 0, 0, tiled=True)
-    moved = lax.all_to_all(by_width, ROW, 0, 0, tiled=True)
-    slots = jnp.zeros((n_col, n_row, col_cells), jnp.float32)
-    for j in range(sib):
-        slots = lax.dynamic_update_slice_in_dim(slots, moved[None, :, j], sibling_columns[j], 0)
+    bit = 1
+    while bit < n_row:
+        pairs = [
+            (r * n_col + k, (r ^ bit) * n_col + (k + r - (r ^ bit)) % n_col)
+            for r in range(n_row)
+            for k in range(n_col)
+        ]
+        inner = inner + lax.ppermute(inner, ROW + COL, pairs)
+        bit *= 2
+    slots = pl.pallas_call(
+        slots_kernel,
+        out_shape=jax.ShapeDtypeStruct((n_col, width // n_row, row_cells + width), jnp.float32),
+        in_specs=[SMEM] + [VMEM] * 2,
+        out_specs=VMEM,
+        compiler_params=pltpu.CompilerParams(vmem_limit_bytes=8 << 20),
+    )(table, moved, inner)
     gathered = lax.all_to_all(slots, COL, 0, 0, tiled=True)
-    inner = jnp.einsum(
-        "rjt,jtv->jrv",
-        moved,
-        panels.reshape(sib, row_cells, width),
-        precision=lax.Precision.HIGH,
-        preferred_element_type=jnp.float32,
-    )
-    inner = inner + swapped(inner, "row_1", 1)
-    for step in (1, 2, 4):
-        inner = inner + swapped(inner, "row_0", step)
-    gathered, inner = lax.optimization_barrier((gathered, inner))
-    diag_slots = jnp.zeros((n_col, n_row, width), jnp.float32)
-    for j in range(sib):
-        diag_slots = lax.dynamic_update_slice_in_dim(
-            diag_slots, inner[j][None], sibling_columns[j], 0
-        )
-    diag_parts = lax.all_to_all(diag_slots, COL, 0, 0, tiled=True)
-    lower_out = gathered.transpose(2, 1, 0).reshape(1, row_cells, width)
-    diag_total = diag_parts.transpose(1, 0, 2).reshape(width, width)
-    present = jnp.sum((sibling_columns == col_index).astype(jnp.float32))
-    diag_out = (present * diag_inv[0] - diag_total)[None]
-    return (upper_part, lower_out, diag_out)
+    lower, diag = pl.pallas_call(
+        finish_kernel,
+        out_shape=(
+            jax.ShapeDtypeStruct((row_cells, width), jnp.float32),
+            jax.ShapeDtypeStruct((width, width), jnp.float32),
+        ),
+        in_specs=[SMEM] + [VMEM] * 2,
+        out_specs=(VMEM, VMEM),
+        compiler_params=pltpu.CompilerParams(vmem_limit_bytes=12 << 20),
+    )(table, gathered, diag_inv[0])
+    return (upper_part, lower[None], diag[None])
 
 
 def solution(mesh):

time: 252 us -> 241 us (0.956)
  waiting for transfers between devices: 114 us -> 77.5 us
  starting transfers between devices: 50.4 us -> 83 us
  between operations: 22.6 us -> 2.18 us
  blocking collectives: 13.6 us -> 29.1 us
  local copies, waits for them, and re-layouts: 21 us -> 6.71 us
  other arithmetic: 9.66 us -> 19.8 us
  Pallas kernels: 17.7 us -> 22.4 us
  matrix products: 3.91 us -> 0 us
    reduce_scatter x1 -> x0, waiting for transfers between devices: 57.9 us -> none  [listed_products(): near = lax.psum_scatter(u, 'row_0', scatter_dimension=0, tiled=True)[0]]
    ppermute x0 -> x6, starting transfers between devices: none -> 34.3 us  [the longest x4 16 us: per_device(): inner = inner + lax.ppermute(inner, ROW + COL, pairs)]
    ppermute x6 -> x20, waiting for transfers between devices: 4.28 us -> 34.6 us  [turned(): lax.ppermute(x, axis, [(i, (i + shift) % length) for i in range(length)])]
    ppermute x0 -> x6, waiting for transfers between devices: none -> 23.6 us  [the longest x4 15.6 us: per_device(): inner = inner + lax.ppermute(inner, ROW + COL, pairs)]
    ppermute x6 -> x20, starting transfers between devices: 6.51 us -> 29.5 us  [turned(): lax.ppermute(x, axis, [(i, (i + shift) % length) for i in range(length)])]
    all_to_all x3 -> x0, starting transfers between devices: 23 us -> none  [the longest x1 10.1 us: per_device(): diag_parts = lax.all_to_all(diag_slots, COL, 0, 0, tiled=True)]
    ppermute x8 -> x4, waiting for transfers between devices: 32.7 us -> 11.6 us  [swapped(): return lax.ppermute(x, axis, [(i, i ^ bit) for i in range(length)])]
    all_to_all x1, blocking collectives: 13.6 us -> 29.1 us  [per_device(): gathered = lax.all_to_all(slots, COL, 0, 0, tiled=True)]
  transfers between devices with their start and end apart: 19 -> 31, of which waited for: 13 -> 22; matrix products, arithmetic and copies ran while one was open for 6% -> 5% of each run, Pallas kernels for 2% -> 0%
where the time goes in v4:
time: 241 us
  starting transfers between devices  83 us (34%)
  waiting for transfers between devices  77.5 us (32%)
  blocking collectives  29.1 us (12%)
  Pallas kernels  22.4 us (9%)
  other arithmetic  19.8 us (8%)
  local copies, waits for them, and re-layouts  6.71 us (3%)
    ppermute x20, waiting for transfers between devices, turned(): lax.ppermute(x, axis, [(i, (i + shift) % length) for i in range(length)])  34.6 us
    ppermute x20, starting transfers between devices, turned(): lax.ppermute(x, axis, [(i, (i + shift) % length) for i in range(length)])  29.5 us
    all_to_all x1, blocking collectives, per_device(): gathered = lax.all_to_all(slots, COL, 0, 0, tiled=True)  29.1 us
    ppermute x4, starting transfers between devices, per_device(): inner = inner + lax.ppermute(inner, ROW + COL, pairs)  16 us
    ppermute x4, waiting for transfers between devices, per_device(): inner = inner + lax.ppermute(inner, ROW + COL, pairs)  15.6 us
    pallas_call x1, Pallas kernels, listed_products(): pl.pallas_call(functools.partial(product_kernel, cap, sib), out_shape=(ja...  13.4 us
    ppermute x4, starting transfers between devices, swapped(): return lax.ppermute(x, axis, [(i, i ^ bit) for i in range(length)])  12.2 us
    ppermute x4, waiting for transfers between devices, swapped(): return lax.ppermute(x, axis, [(i, i ^ bit) for i in range(length)])  11.6 us
  transfers between devices with their start and end apart: 31, of which 22 were waited for; matrix products, arithmetic and copies ran while one was open for 5% of the time, Pallas kernels for 0%

profile of v4, /device:TPU:1, one launch (start us, length us, event | category | flops | bytes accessed | tf_op | source)
XLA Modules:
  0.0 241.0 jit_solution(5622015245517130559)
XLA Ops:
  0.6 2.5 %copy.12 = f32[16,10,8,256]{3,2,1,0:T(8,128)} copy(f32[16,10,8,256]{3,2,0,1:T(8,128)} %bitcast.98) | data formatting | bytes 2621440 | tf_op jit(solution)/shard_map/transpose | solution.py:331
  3.1 7.0 %all-to-all-start.2 = ((f32[16,10,8,256]{3,2,1,0:T(8,128)}), f32[16,10,8,256]{3,2,1,0:T(8,128)S(1)}, u32[]{:S(2)}, u32[]{:S(2)}) async-start(f32[16,10,8,256]{3,2,1,0:T(8,128)} %copy.12), calls=%async_computation.2 | async-start | bytes 2621440 | tf_op jit(solution)/shard_map/all_to_all | solution.py:332
  14.6 6.5 %fusion.16 = (bf16[1280,1280]{1,0:T(8,128)(2,1)}, bf16[1280,1280]{1,0:T(8,128)(2,1)}) fusion(f32[1280,1280]{1,0:T(8,128)} %param.8), kind=kLoop, calls=%fused_computation.72 | loop fusion | flops 6553600 | bytes 13107200 | tf_op jit(solution)/shard_map/convert_element_type | solution.py:335
  21.1 7.7 %all-to-all-done.2 = f32[16,10,8,256]{3,2,1,0:T(8,128)S(1)} async-done(((f32[16,10,8,256]{3,2,1,0:T(8,128)}), f32[16,10,8,256]{3,2,1,0:T(8,128)S(1)}, u32[]{:S(2)}, u32[]{:S(2)}) %all-to-all-start.2) | async-done | bytes 1310752 | tf_op jit(solution)/shard_map/all_to_all | solution.py:332
  28.8 148.5 %conditional.1 = (f32[4,16,1280]{2,1,0:T(8,128)S(1)}, f32[4,16,1280]{2,1,0:T(8,128)S(1)}, f32[4,16,256]{2,1,0:T(8,128)S(1)}) conditional(s32[]{:T(128)} %clamp.3, (f32[16,10,8,256]{3,2,1,0:T(8,128)S(1)}, s32[362]{0:T(512)S(1)}, bf16[1280,1280]{1,0:T(8,128)(2,1)}, bf16[1280,1280]{1,0:T(8,128)(2,1)}) %tuple.16, (f32[16,10,8,256]{3,2,1,0:T(8,128)S(1)}, ...), branch_computations={%region_12.13_spmd, %region_13.15_spmd} | conditional | flops 10567844 | bytes 131860560 | solution.py:370
  28.8 0.7 branch_0_fun.5
  30.1 5.9 %collective-permute-done = f32[28,8,256]{2,1,0:T(8,128)S(1)} collective-permute-done((f32[28,8,256]{2,1,0:T(8,128)S(1)}, f32[28,8,256]{2,1,0:T(8,128)S(1)}, u32[]{:S(2)}, u32[]{:S(2)}) %collective-permute-start) | collective-permute-done | bytes 229408 | tf_op jit(solution)/shard_map/cond/branch_0_fun/ppermute | solution.py:26
  36.0 1.4 collective-permute-start.4
  37.8 1.1 collective-permute-start.3
  39.0 2.5 %collective-permute-done.4 = f32[28,8,256]{2,1,0:T(8,128)S(1)} collective-permute-done((f32[28,8,256]{2,1,0:T(8,128)S(1)}, f32[28,8,256]{2,1,0:T(8,128)S(1)}, u32[]{:S(2)}, u32[]{:S(2)}) %collective-permute-start.4) | collective-permute-done | bytes 229408 | tf_op jit(solution)/shard_map/cond/branch_0_fun/ppermute | solution.py:31
  41.5 3.4 %collective-permute-start.6 = (f32[28,8,256]{2,1,0:T(8,128)S(1)}, f32[28,8,256]{2,1,0:T(8,128)S(1)}, u32[]{:S(2)}, u32[]{:S(2)}) collective-permute-start(f32[28,8,256]{2,1,0:T(8,128)S(1)} %collective-permute-done.4), channel_id=1, source_target_pairs={{0,6},{2,0},{4,2},{6,4},{1,7},{3,1},{5,3},{7,5},{8,14},{10,8},{12,... | collective-permute-start | bytes 688136 | tf_op jit(solution)/shard_map/cond/branch_0_fun/ppermute | solution.py:31
  44.9 1.5 collective-permute-done.2
  46.5 4.7 %collective-permute-start.7 = (f32[4,28,8,256]{3,2,1,0:T(8,128)S(1)}, f32[4,28,8,256]{3,2,1,0:T(8,128)S(1)}, u32[]{:S(2)}, u32[]{:S(2)}) collective-permute-start(f32[4,28,8,256]{3,2,1,0:T(8,128)S(1)} %pad_maximum_fusion.g0), channel_id=1, source_target_pairs={{0,1},{1,0},{2,3},{3,2},{4,5},{5,4},{6,7},{7,6},{8,9},{9,8},{10,11... | collective-permute-start | bytes 2752520 | tf_op jit(solution)/shard_map/cond/branch_0_fun/ppermute | solution.py:26
  51.4 2.6 %collective-permute-start.8 = (f32[4,28,8,256]{3,2,1,0:T(8,128)S(1)}, f32[4,28,8,256]{3,2,1,0:T(8,128)}, u32[]{:S(2)}, u32[]{:S(2)}) collective-permute-start(f32[4,28,8,256]{3,2,1,0:T(8,128)S(1)} %pad_maximum_fusion.1.g1), channel_id=1, source_target_pairs={{0,1},{1,0},{2,3},{3,2},{4,5},{5,4},{6,7},{7,6},{8,9},{9,8},{10,11... | collective-permute-start | bytes 2752520 | tf_op jit(solution)/shard_map/cond/branch_0_fun/ppermute | solution.py:26
  54.0 2.2 collective-permute-done.8.c1
  56.3 13.4 %branch_0_fun.6 = (f32[8,28,32,128]{3,2,1,0:T(8,128)S(1)}, f32[28,128,256]{2,1,0:T(8,128)S(1)}) custom-call(s32[362]{0:T(512)S(1)} %get-tuple-element.16.tab, f32[4,28,8,256]{3,2,1,0:T(8,128)S(1)} %pad_maximum_fusion.g0, f32[4,28,8,256]{3,2,1,0:T(8,128)S(1)} %pad_maximum_fusion.1.g1, f32[4,28,8,256]{3,2,1,0:T(8,128)S(1)} %collective-permute-done.7.c0, ...), custom_call_target="tpu_custom_call" | custom-call | tf_op jit(solution)/shard_map/cond/branch_0_fun/pallas_call | solution.py:251
  69.7 1.8 copy-done.1
  71.5 1.8 copy-done.2
  73.3 5.8 %collective-permute-start.16 = (f32[14,32,128]{2,1,0:T(8,128)S(1)}, f32[14,32,128]{2,1,0:T(8,128)S(1)}, u32[]{:S(2)}, u32[]{:S(2)}) collective-permute-start(f32[14,32,128]{2,1,0:T(8,128)S(1)} %get-tuple-element.72), channel_id=1, source_target_pairs={{0,224},{32,0},{64,32},{96,64},{128,96},{160,128},{192,160},{224,1... | collective-permute-start | bytes 688136 | tf_op jit(solution)/shard_map/cond/branch_0_fun/ppermute | solution.py:31
  79.1 3.0 %collective-permute-done.16 = f32[14,32,128]{2,1,0:T(8,128)S(1)} collective-permute-done((f32[14,32,128]{2,1,0:T(8,128)S(1)}, f32[14,32,128]{2,1,0:T(8,128)S(1)}, u32[]{:S(2)}, u32[]{:S(2)}) %collective-permute-start.16) | collective-permute-done | bytes 229408 | tf_op jit(solution)/shard_map/cond/branch_0_fun/ppermute | solution.py:31
  82.1 3.1 %collective-permute-done.9 = f32[14,32,128]{2,1,0:T(8,128)S(1)} collective-permute-done((f32[14,32,128]{2,1,0:T(8,128)S(1)}, f32[14,32,128]{2,1,0:T(8,128)S(1)}, u32[]{:S(2)}, u32[]{:S(2)}) %collective-permute-start.9) | collective-permute-done | bytes 229408 | tf_op jit(solution)/shard_map/cond/branch_0_fun/ppermute | solution.py:31
  85.2 1.1 fusion.14
  86.4 2.7 %collective-permute-start.17 = (f32[14,32,128]{2,1,0:T(8,128)S(1)}, f32[14,32,128]{2,1,0:T(8,128)S(1)}, u32[]{:S(2)}, u32[]{:S(2)}) collective-permute-start(f32[14,32,128]{2,1,0:T(8,128)S(1)} %get-tuple-element.70), channel_id=1, source_target_pairs={{0,224},{32,0},{64,32},{96,64},{128,96},{160,128},{192,160},{224,1... | collective-permute-start | bytes 688136 | tf_op jit(solution)/shard_map/cond/branch_0_fun/ppermute | solution.py:31
  89.1 3.4 %collective-permute-done.10 = f32[14,32,128]{2,1,0:T(8,128)S(1)} collective-permute-done((f32[14,32,128]{2,1,0:T(8,128)S(1)}, f32[14,32,128]{2,1,0:T(8,128)S(1)}, u32[]{:S(2)}, u32[]{:S(2)}) %collective-permute-start.10) | collective-permute-done | bytes 229408 | tf_op jit(solution)/shard_map/cond/branch_0_fun/ppermute | solution.py:31
  92.5 1.1 fusion.13
  93.7 2.7 %collective-permute-start.18 = (f32[14,32,128]{2,1,0:T(8,128)S(1)}, f32[14,32,128]{2,1,0:T(8,128)S(1)}, u32[]{:S(2)}, u32[]{:S(2)}) collective-permute-start(f32[14,32,128]{2,1,0:T(8,128)S(1)} %get-tuple-element.68), channel_id=1, source_target_pairs={{0,224},{32,0},{64,32},{96,64},{128,96},{160,128},{192,160},{224,1... | collective-permute-start | bytes 688136 | tf_op jit(solution)/shard_map/cond/branch_0_fun/ppermute | solution.py:31
  96.5 3.3 %collective-permute-done.11 = f32[14,32,128]{2,1,0:T(8,128)S(1)} collective-permute-done((f32[14,32,128]{2,1,0:T(8,128)S(1)}, f32[14,32,128]{2,1,0:T(8,128)S(1)}, u32[]{:S(2)}, u32[]{:S(2)}) %collective-permute-start.11) | collective-permute-done | bytes 229408 | tf_op jit(solution)/shard_map/cond/branch_0_fun/ppermute | solution.py:31
  99.8 1.1 fusion.12
  101.0 2.8 %collective-permute-start.19 = (f32[14,32,128]{2,1,0:T(8,128)S(1)}, f32[14,32,128]{2,1,0:T(8,128)S(1)}, u32[]{:S(2)}, u32[]{:S(2)}) collective-permute-start(f32[14,32,128]{2,1,0:T(8,128)S(1)} %get-tuple-element.66), channel_id=1, source_target_pairs={{0,224},{32,0},{64,32},{96,64},{128,96},{160,128},{192,160},{224,1... | collective-permute-start | bytes 688136 | tf_op jit(solution)/shard_map/cond/branch_0_fun/ppermute | solution.py:31
  103.8 3.3 %collective-permute-done.12 = f32[14,32,128]{2,1,0:T(8,128)S(1)} collective-permute-done((f32[14,32,128]{2,1,0:T(8,128)S(1)}, f32[14,32,128]{2,1,0:T(8,128)S(1)}, u32[]{:S(2)}, u32[]{:S(2)}) %collective-permute-start.12) | collective-permute-done | bytes 229408 | tf_op jit(solution)/shard_map/cond/branch_0_fun/ppermute | solution.py:31
  107.2 1.1 fusion.11
  108.3 1.4 collective-permute-start.13
  109.7 1.8 collective-permute-start.20
  111.4 4.3 %collective-permute-done.13 = f32[14,32,128]{2,1,0:T(8,128)S(1)} collective-permute-done((f32[14,32,128]{2,1,0:T(8,128)S(1)}, f32[14,32,128]{2,1,0:T(8,128)S(1)}, u32[]{:S(2)}, u32[]{:S(2)}) %collective-permute-start.13) | collective-permute-done | bytes 229408 | tf_op jit(solution)/shard_map/cond/branch_0_fun/ppermute | solution.py:31
  115.8 1.3 collective-permute-done.20
  117.1 1.1 fusion.10
  118.2 1.2 collective-permute-start.14
  119.5 1.5 collective-permute-start.21
  121.0 4.8 %collective-permute-done.14 = f32[14,32,128]{2,1,0:T(8,128)S(1)} collective-permute-done((f32[14,32,128]{2,1,0:T(8,128)S(1)}, f32[14,32,128]{2,1,0:T(8,128)S(1)}, u32[]{:S(2)}, u32[]{:S(2)}) %collective-permute-start.14) | collective-permute-done | bytes 229408 | tf_op jit(solution)/shard_map/cond/branch_0_fun/ppermute | solution.py:31
  125.8 1.1 fusion.9
  126.9 1.2 collective-permute-start.15
  128.1 1.6 collective-permute-start.22
  129.6 3.9 %collective-permute-done.15 = f32[14,32,128]{2,1,0:T(8,128)S(1)} collective-permute-done((f32[14,32,128]{2,1,0:T(8,128)S(1)}, f32[14,32,128]{2,1,0:T(8,128)S(1)}, u32[]{:S(2)}, u32[]{:S(2)}) %collective-permute-start.15) | collective-permute-done | bytes 229408 | tf_op jit(solution)/shard_map/cond/branch_0_fun/ppermute | solution.py:31
  133.5 1.1 fusion.8
  134.7 4.5 %collective-permute-start.23 = (f32[28,16,128]{2,1,0:T(8,128)S(1)}, f32[28,16,128]{2,1,0:T(8,128)S(1)}, u32[]{:S(2)}, u32[]{:S(2)}) collective-permute-start(f32[28,16,128]{2,1,0:T(8,128)S(1)} %pad_maximum_fusion.2), channel_id=1, source_target_pairs={{0,16},{16,0},{1,17},{17,1},{2,18},{18,2},{3,19},{19,3},{4,20},{20... | collective-permute-start | bytes 688136 | tf_op jit(solution)/shard_map/cond/branch_0_fun/ppermute | solution.py:26
  139.2 3.4 %collective-permute-done.23 = f32[28,16,128]{2,1,0:T(8,128)S(1)} collective-permute-done((f32[28,16,128]{2,1,0:T(8,128)S(1)}, f32[28,16,128]{2,1,0:T(8,128)S(1)}, u32[]{:S(2)}, u32[]{:S(2)}) %collective-permute-start.23) | collective-permute-done | bytes 229408 | tf_op jit(solution)/shard_map/cond/branch_0_fun/ppermute | solution.py:26
  142.6 7.5 %collective-permute-start.24 = (f32[28,16,128]{2,1,0:T(8,128)S(1)}, f32[28,16,128]{2,1,0:T(8,128)S(1)}, u32[]{:S(2)}, u32[]{:S(2)}) collective-permute-start(f32[28,16,128]{2,1,0:T(8,128)S(1)} %maximum_add_fusion.x_ref), channel_id=1, source_target_pairs={{0,0},{1,15},{2,14},{3,13},{4,12},{5,11},{6,10},{7,9},{8,8},{9,7},... | collective-permute-start | bytes 688136 | tf_op jit(solution)/shard_map/cond/branch_0_fun/ppermute | solution.py:293
  150.2 3.6 %collective-permute-done.24 = f32[28,16,128]{2,1,0:T(8,128)S(1)} collective-permute-done((f32[28,16,128]{2,1,0:T(8,128)S(1)}, f32[28,16,128]{2,1,0:T(8,128)S(1)}, u32[]{:S(2)}, u32[]{:S(2)}) %collective-permute-start.24) | collective-permute-done | bytes 229408 | tf_op jit(solution)/shard_map/cond/branch_0_fun/ppermute | solution.py:293
  153.8 10.8 %collective-permute-start.25 = (f32[28,16,128]{2,1,0:T(8,128)S(1)}, f32[28,16,128]{2,1,0:T(8,128)S(1)}, u32[]{:S(2)}, u32[]{:S(2)}) collective-permute-start(f32[28,16,128]{2,1,0:T(8,128)S(1)} %collective-permute-done.24), channel_id=1, source_target_pairs={{0,0},{1,241},{2,226},{3,211},{4,196},{5,181},{6,166},{7,151},{8,1... | collective-permute-start | bytes 688136 | tf_op jit(solution)/shard_map/cond/branch_0_fun/ppermute | solution.py:293
  164.6 2.8 %fusion = (bf16[28,128,256]{2,1,0:T(8,128)(2,1)S(1)}, bf16[28,128,256]{2,1,0:T(8,128)(2,1)S(1)}) fusion(f32[28,128,256]{2,1,0:T(8,128)} %copy-done.1), kind=kLoop, calls=%fused_computation.2 | loop fusion | flops 3670016 | bytes 7340032 | tf_op jit(solution)/shard_map/cond/branch_0_fun/convert_element_type | solution.py:295
  167.4 0.7 branch_0_fun.7
  168.1 4.3 %collective-permute-done.25.x_ref = f32[28,16,128]{2,1,0:T(8,128)S(1)} collective-permute-done((f32[28,16,128]{2,1,0:T(8,128)S(1)}, f32[28,16,128]{2,1,0:T(8,128)S(1)}, u32[]{:S(2)}, u32[]{:S(2)}) %collective-permute-start.25) | collective-permute-done | bytes 229408 | tf_op jit(solution)/shard_map/cond/branch_0_fun/ppermute | solution.py:293
  173.1 4.1 %branch_0_fun.9 = f32[4,16,256]{2,1,0:T(8,128)S(1)} custom-call(s32[362]{0:T(512)S(1)} %get-tuple-element.16.tab, f32[28,16,128]{2,1,0:T(8,128)S(1)} %collective-permute-done.25.x_ref, bf16[28,128,256]{2,1,0:T(8,128)(2,1)S(1)} %get-tuple-element.56.hi_ref, bf16[28,128,256]{2,1,0:T(8,128)(2,1)S(1)} %get-tuple-element.55.lo_ref), custom_call_target="tpu_custom_call" | custom-call | tf_op jit(solution)/shard_map/cond/branch_0_fun/pallas_call | solution.py:296
  177.3 7.7 %collective-permute-start.29 = (f32[4,16,256]{2,1,0:T(8,128)S(1)}, f32[4,16,256]{2,1,0:T(8,128)S(1)}, u32[]{:S(2)}, u32[]{:S(2)}) collective-permute-start(f32[4,16,256]{2,1,0:T(8,128)S(1)} %get-tuple-element.38), channel_id=1, source_target_pairs={{0,31},{1,16},{2,17},{3,18},{4,19},{5,20},{6,21},{7,22},{8,23},{9,... | collective-permute-start | bytes 196616 | tf_op jit(solution)/shard_map/ppermute | solution.py:385
  185.1 2.0 collective-permute-done.29
  187.1 1.8 collective-permute-start.30
  188.8 4.4 %collective-permute-done.30 = f32[4,16,256]{2,1,0:T(8,128)S(1)} collective-permute-done((f32[4,16,256]{2,1,0:T(8,128)S(1)}, f32[4,16,256]{2,1,0:T(8,128)S(1)}, u32[]{:S(2)}, u32[]{:S(2)}) %collective-permute-start.30) | collective-permute-done | bytes 65568 | tf_op jit(solution)/shard_map/ppermute | solution.py:385
  193.3 2.3 collective-permute-start.31
  195.5 5.5 %collective-permute-done.31 = f32[4,16,256]{2,1,0:T(8,128)S(1)} collective-permute-done((f32[4,16,256]{2,1,0:T(8,128)S(1)}, f32[4,16,256]{2,1,0:T(8,128)S(1)}, u32[]{:S(2)}, u32[]{:S(2)}) %collective-permute-start.31) | collective-permute-done | bytes 65568 | tf_op jit(solution)/shard_map/ppermute | solution.py:385
  201.0 4.3 %collective-permute-start.32 = (f32[4,16,256]{2,1,0:T(8,128)S(1)}, f32[4,16,256]{2,1,0:T(8,128)S(1)}, u32[]{:S(2)}, u32[]{:S(2)}) collective-permute-start(f32[4,16,256]{2,1,0:T(8,128)S(1)} %add.740), channel_id=1, source_target_pairs={{0,136},{1,137},{2,138},{3,139},{4,140},{5,141},{6,142},{7,143},{8... | collective-permute-start | bytes 196616 | tf_op jit(solution)/shard_map/ppermute | solution.py:385
  205.3 3.8 %collective-permute-done.32 = f32[4,16,256]{2,1,0:T(8,128)S(1)} collective-permute-done((f32[4,16,256]{2,1,0:T(8,128)S(1)}, f32[4,16,256]{2,1,0:T(8,128)S(1)}, u32[]{:S(2)}, u32[]{:S(2)}) %collective-permute-start.32) | collective-permute-done | bytes 65568 | tf_op jit(solution)/shard_map/ppermute | solution.py:385
  209.1 0.7 shard_map.85
  209.8 29.1 %all_to_all.18.x_ref = f32[16,16,1536]{2,1,0:T(8,128)S(1)} all-to-all(f32[16,16,1536]{2,1,0:T(8,128)S(1)} %shard_map.85), channel_id=1, replica_groups=mesh['row_0'=8,'row_1'=2,'col_y'=2,'col_x'=4,'core'=2] {'col_y','col_x',..., dimensions={0} | all-to-all | bytes 3145728 | tf_op jit(solution)/shard_map/all_to_all | solution.py:394
  238.9 2.0 shard_map.86
  (74 shorter events, 5.3 us)
Async XLA Ops:
  3.1 7.0 %copy-start.8 = (s32[4]{0:T(128)S(1)}, s32[4]{0:T(128)}, u32[]{:S(2)}) copy-start(s32[4]{0:T(128)} %param.12) | copy-start | bytes 52
  3.1 7.0 %copy-start.7 = (s32[4,96]{1,0:T(4,128)S(1)}, s32[4,96]{1,0:T(4,128)}, u32[]{:S(2)}) copy-start(s32[4,96]{1,0:T(4,128)} %param.11) | copy-start | bytes 4612
  3.1 7.9 %copy-start.9 = (s32[4]{0:T(128)S(1)}, s32[4]{0:T(128)}, u32[]{:S(2)}) copy-start(s32[4]{0:T(128)} %param.13) | copy-start | bytes 52
  3.1 25.6 %all-to-all-start.2 = ((f32[16,10,8,256]{3,2,1,0:T(8,128)}), f32[16,10,8,256]{3,2,1,0:T(8,128)S(1)}, u32[]{:S(2)}, u32[]{:S(2)}) async-start(f32[16,10,8,256]{3,2,1,0:T(8,128)} %copy.12), calls=%async_computation.2 | async-start | bytes 2621440 | tf_op jit(solution)/shard_map/all_to_all | solution.py:332
  29.5 6.5 %collective-permute-start = (f32[28,8,256]{2,1,0:T(8,128)S(1)}, f32[28,8,256]{2,1,0:T(8,128)S(1)}, u32[]{:S(2)}, u32[]{:S(2)}) collective-permute-start(f32[28,8,256]{2,1,0:T(8,128)S(1)} %branch_0_fun.5), channel_id=1, source_target_pairs={{0,8},{8,0},{1,9},{9,1},{2,10},{10,2},{3,11},{11,3},{4,12},{12,4},... | collective-permute-start | bytes 688136 | tf_op jit(solution)/shard_map/cond/branch_0_fun/ppermute | solution.py:26
  29.9 9.1 %collective-permute-start.1 = (f32[28,8,256]{2,1,0:T(8,128)S(1)}, f32[28,8,256]{2,1,0:T(8,128)S(1)}, u32[]{:S(2)}, u32[]{:S(2)}) collective-permute-start(f32[28,8,256]{2,1,0:T(8,128)S(1)} %branch_0_fun.5), channel_id=1, source_target_pairs={{0,2},{2,4},{4,6},{6,0},{1,3},{3,5},{5,7},{7,1},{8,10},{10,12},{12... | collective-permute-start | bytes 688136 | tf_op jit(solution)/shard_map/cond/branch_0_fun/ppermute | solution.py:31
  36.0 5.5 %collective-permute-start.4 = (f32[28,8,256]{2,1,0:T(8,128)S(1)}, f32[28,8,256]{2,1,0:T(8,128)S(1)}, u32[]{:S(2)}, u32[]{:S(2)}) collective-permute-start(f32[28,8,256]{2,1,0:T(8,128)S(1)} %collective-permute-done), channel_id=1, source_target_pairs={{0,6},{2,0},{4,2},{6,4},{1,7},{3,1},{5,3},{7,5},{8,14},{10,8},{12,... | collective-permute-start | bytes 688136 | tf_op jit(solution)/shard_map/cond/branch_0_fun/ppermute | solution.py:31
  37.5 9.0 %collective-permute-start.2 = (f32[28,8,256]{2,1,0:T(8,128)S(1)}, f32[28,8,256]{2,1,0:T(8,128)S(1)}, u32[]{:S(2)}, u32[]{:S(2)}) collective-permute-start(f32[28,8,256]{2,1,0:T(8,128)S(1)} %branch_0_fun.5), channel_id=1, source_target_pairs={{0,6},{2,0},{4,2},{6,4},{1,7},{3,1},{5,3},{7,5},{8,14},{10,8},{12,... | collective-permute-start | bytes 688136 | tf_op jit(solution)/shard_map/cond/branch_0_fun/ppermute | solution.py:31
  37.8 13.5 %collective-permute-start.3 = (f32[28,8,256]{2,1,0:T(8,128)S(1)}, f32[28,8,256]{2,1,0:T(8,128)S(1)}, u32[]{:S(2)}, u32[]{:S(2)}) collective-permute-start(f32[28,8,256]{2,1,0:T(8,128)S(1)} %collective-permute-done), channel_id=1, source_target_pairs={{0,2},{2,4},{4,6},{6,0},{1,3},{3,5},{5,7},{7,1},{8,10},{10,12},{12... | collective-permute-start | bytes 688136 | tf_op jit(solution)/shard_map/cond/branch_0_fun/ppermute | solution.py:31
  38.9 12.3 %collective-permute-start.5 = (f32[28,8,256]{2,1,0:T(8,128)S(1)}, f32[28,8,256]{2,1,0:T(8,128)S(1)}, u32[]{:S(2)}, u32[]{:S(2)}) collective-permute-start(f32[28,8,256]{2,1,0:T(8,128)S(1)} %collective-permute-done.1), channel_id=1, source_target_pairs={{0,2},{2,4},{4,6},{6,0},{1,3},{3,5},{5,7},{7,1},{8,10},{10,12},{12... | collective-permute-start | bytes 688136 | tf_op jit(solution)/shard_map/cond/branch_0_fun/ppermute | solution.py:31
  41.5 9.8 %collective-permute-start.6 = (f32[28,8,256]{2,1,0:T(8,128)S(1)}, f32[28,8,256]{2,1,0:T(8,128)S(1)}, u32[]{:S(2)}, u32[]{:S(2)}) collective-permute-start(f32[28,8,256]{2,1,0:T(8,128)S(1)} %collective-permute-done.4), channel_id=1, source_target_pairs={{0,6},{2,0},{4,2},{6,4},{1,7},{3,1},{5,3},{7,5},{8,14},{10,8},{12,... | collective-permute-start | bytes 688136 | tf_op jit(solution)/shard_map/cond/branch_0_fun/ppermute | solution.py:31
  46.5 7.5 %collective-permute-start.7 = (f32[4,28,8,256]{3,2,1,0:T(8,128)S(1)}, f32[4,28,8,256]{3,2,1,0:T(8,128)S(1)}, u32[]{:S(2)}, u32[]{:S(2)}) collective-permute-start(f32[4,28,8,256]{3,2,1,0:T(8,128)S(1)} %pad_maximum_fusion.g0), channel_id=1, source_target_pairs={{0,1},{1,0},{2,3},{3,2},{4,5},{5,4},{6,7},{7,6},{8,9},{9,8},{10,11... | collective-permute-start | bytes 2752520 | tf_op jit(solution)/shard_map/cond/branch_0_fun/ppermute | solution.py:26
  51.4 4.8 %collective-permute-start.8 = (f32[4,28,8,256]{3,2,1,0:T(8,128)S(1)}, f32[4,28,8,256]{3,2,1,0:T(8,128)}, u32[]{:S(2)}, u32[]{:S(2)}) collective-permute-start(f32[4,28,8,256]{3,2,1,0:T(8,128)S(1)} %pad_maximum_fusion.1.g1), channel_id=1, source_target_pairs={{0,1},{1,0},{2,3},{3,2},{4,5},{5,4},{6,7},{7,6},{8,9},{9,8},{10,11... | collective-permute-start | bytes 2752520 | tf_op jit(solution)/shard_map/cond/branch_0_fun/ppermute | solution.py:26
  69.7 1.8 copy-start.1
  71.5 1.8 copy-start.2
  73.3 8.8 %collective-permute-start.16 = (f32[14,32,128]{2,1,0:T(8,128)S(1)}, f32[14,32,128]{2,1,0:T(8,128)S(1)}, u32[]{:S(2)}, u32[]{:S(2)}) collective-permute-start(f32[14,32,128]{2,1,0:T(8,128)S(1)} %get-tuple-element.72), channel_id=1, source_target_pairs={{0,224},{32,0},{64,32},{96,64},{128,96},{160,128},{192,160},{224,1... | collective-permute-start | bytes 688136 | tf_op jit(solution)/shard_map/cond/branch_0_fun/ppermute | solution.py:31
  79.1 6.1 %collective-permute-start.9 = (f32[14,32,128]{2,1,0:T(8,128)S(1)}, f32[14,32,128]{2,1,0:T(8,128)S(1)}, u32[]{:S(2)}, u32[]{:S(2)}) collective-permute-start(f32[14,32,128]{2,1,0:T(8,128)S(1)} %get-tuple-element.71), channel_id=1, source_target_pairs={{0,32},{32,64},{64,96},{96,128},{128,160},{160,192},{192,224},{224... | collective-permute-start | bytes 688136 | tf_op jit(solution)/shard_map/cond/branch_0_fun/ppermute | solution.py:31
  86.3 6.2 %collective-permute-start.10 = (f32[14,32,128]{2,1,0:T(8,128)S(1)}, f32[14,32,128]{2,1,0:T(8,128)S(1)}, u32[]{:S(2)}, u32[]{:S(2)}) collective-permute-start(f32[14,32,128]{2,1,0:T(8,128)S(1)} %get-tuple-element.69), channel_id=1, source_target_pairs={{0,32},{32,64},{64,96},{96,128},{128,160},{160,192},{192,224},{224... | collective-permute-start | bytes 688136 | tf_op jit(solution)/shard_map/cond/branch_0_fun/ppermute | solution.py:31
  86.4 6.1 %collective-permute-start.17 = (f32[14,32,128]{2,1,0:T(8,128)S(1)}, f32[14,32,128]{2,1,0:T(8,128)S(1)}, u32[]{:S(2)}, u32[]{:S(2)}) collective-permute-start(f32[14,32,128]{2,1,0:T(8,128)S(1)} %get-tuple-element.70), channel_id=1, source_target_pairs={{0,224},{32,0},{64,32},{96,64},{128,96},{160,128},{192,160},{224,1... | collective-permute-start | bytes 688136 | tf_op jit(solution)/shard_map/cond/branch_0_fun/ppermute | solution.py:31
  93.6 6.2 %collective-permute-start.11 = (f32[14,32,128]{2,1,0:T(8,128)S(1)}, f32[14,32,128]{2,1,0:T(8,128)S(1)}, u32[]{:S(2)}, u32[]{:S(2)}) collective-permute-start(f32[14,32,128]{2,1,0:T(8,128)S(1)} %get-tuple-element.67), channel_id=1, source_target_pairs={{0,32},{32,64},{64,96},{96,128},{128,160},{160,192},{192,224},{224... | collective-permute-start | bytes 688136 | tf_op jit(solution)/shard_map/cond/branch_0_fun/ppermute | solution.py:31
  93.7 6.1 %collective-permute-start.18 = (f32[14,32,128]{2,1,0:T(8,128)S(1)}, f32[14,32,128]{2,1,0:T(8,128)S(1)}, u32[]{:S(2)}, u32[]{:S(2)}) collective-permute-start(f32[14,32,128]{2,1,0:T(8,128)S(1)} %get-tuple-element.68), channel_id=1, source_target_pairs={{0,224},{32,0},{64,32},{96,64},{128,96},{160,128},{192,160},{224,1... | collective-permute-start | bytes 688136 | tf_op jit(solution)/shard_map/cond/branch_0_fun/ppermute | solution.py:31
  100.9 6.2 %collective-permute-start.12 = (f32[14,32,128]{2,1,0:T(8,128)S(1)}, f32[14,32,128]{2,1,0:T(8,128)S(1)}, u32[]{:S(2)}, u32[]{:S(2)}) collective-permute-start(f32[14,32,128]{2,1,0:T(8,128)S(1)} %get-tuple-element.65), channel_id=1, source_target_pairs={{0,32},{32,64},{64,96},{96,128},{128,160},{160,192},{192,224},{224... | collective-permute-start | bytes 688136 | tf_op jit(solution)/shard_map/cond/branch_0_fun/ppermute | solution.py:31
  101.0 6.2 %collective-permute-start.19 = (f32[14,32,128]{2,1,0:T(8,128)S(1)}, f32[14,32,128]{2,1,0:T(8,128)S(1)}, u32[]{:S(2)}, u32[]{:S(2)}) collective-permute-start(f32[14,32,128]{2,1,0:T(8,128)S(1)} %get-tuple-element.66), channel_id=1, source_target_pairs={{0,224},{32,0},{64,32},{96,64},{128,96},{160,128},{192,160},{224,1... | collective-permute-start | bytes 688136 | tf_op jit(solution)/shard_map/cond/branch_0_fun/ppermute | solution.py:31
  108.3 7.5 %collective-permute-start.13 = (f32[14,32,128]{2,1,0:T(8,128)S(1)}, f32[14,32,128]{2,1,0:T(8,128)S(1)}, u32[]{:S(2)}, u32[]{:S(2)}) collective-permute-start(f32[14,32,128]{2,1,0:T(8,128)S(1)} %get-tuple-element.63), channel_id=1, source_target_pairs={{0,32},{32,64},{64,96},{96,128},{128,160},{160,192},{192,224},{224... | collective-permute-start | bytes 688136 | tf_op jit(solution)/shard_map/cond/branch_0_fun/ppermute | solution.py:31
  109.7 7.4 %collective-permute-start.20 = (f32[14,32,128]{2,1,0:T(8,128)S(1)}, f32[14,32,128]{2,1,0:T(8,128)S(1)}, u32[]{:S(2)}, u32[]{:S(2)}) collective-permute-start(f32[14,32,128]{2,1,0:T(8,128)S(1)} %get-tuple-element.64), channel_id=1, source_target_pairs={{0,224},{32,0},{64,32},{96,64},{128,96},{160,128},{192,160},{224,1... | collective-permute-start | bytes 688136 | tf_op jit(solution)/shard_map/cond/branch_0_fun/ppermute | solution.py:31
  118.2 7.5 %collective-permute-start.14 = (f32[14,32,128]{2,1,0:T(8,128)S(1)}, f32[14,32,128]{2,1,0:T(8,128)S(1)}, u32[]{:S(2)}, u32[]{:S(2)}) collective-permute-start(f32[14,32,128]{2,1,0:T(8,128)S(1)} %get-tuple-element.61), channel_id=1, source_target_pairs={{0,32},{32,64},{64,96},{96,128},{128,160},{160,192},{192,224},{224... | collective-permute-start | bytes 688136 | tf_op jit(solution)/shard_map/cond/branch_0_fun/ppermute | solution.py:31
  119.5 6.3 %collective-permute-start.21 = (f32[14,32,128]{2,1,0:T(8,128)S(1)}, f32[14,32,128]{2,1,0:T(8,128)S(1)}, u32[]{:S(2)}, u32[]{:S(2)}) collective-permute-start(f32[14,32,128]{2,1,0:T(8,128)S(1)} %get-tuple-element.62), channel_id=1, source_target_pairs={{0,224},{32,0},{64,32},{96,64},{128,96},{160,128},{192,160},{224,1... | collective-permute-start | bytes 688136 | tf_op jit(solution)/shard_map/cond/branch_0_fun/ppermute | solution.py:31
  126.9 6.6 %collective-permute-start.15 = (f32[14,32,128]{2,1,0:T(8,128)S(1)}, f32[14,32,128]{2,1,0:T(8,128)S(1)}, u32[]{:S(2)}, u32[]{:S(2)}) collective-permute-start(f32[14,32,128]{2,1,0:T(8,128)S(1)} %get-tuple-element.59), channel_id=1, source_target_pairs={{0,32},{32,64},{64,96},{96,128},{128,160},{160,192},{192,224},{224... | collective-permute-start | bytes 688136 | tf_op jit(solution)/shard_map/cond/branch_0_fun/ppermute | solution.py:31
  128.1 5.4 %collective-permute-start.22 = (f32[14,32,128]{2,1,0:T(8,128)S(1)}, f32[14,32,128]{2,1,0:T(8,128)S(1)}, u32[]{:S(2)}, u32[]{:S(2)}) collective-permute-start(f32[14,32,128]{2,1,0:T(8,128)S(1)} %get-tuple-element.60), channel_id=1, source_target_pairs={{0,224},{32,0},{64,32},{96,64},{128,96},{160,128},{192,160},{224,1... | collective-permute-start | bytes 688136 | tf_op jit(solution)/shard_map/cond/branch_0_fun/ppermute | solution.py:31
  134.7 7.9 %collective-permute-start.23 = (f32[28,16,128]{2,1,0:T(8,128)S(1)}, f32[28,16,128]{2,1,0:T(8,128)S(1)}, u32[]{:S(2)}, u32[]{:S(2)}) collective-permute-start(f32[28,16,128]{2,1,0:T(8,128)S(1)} %pad_maximum_fusion.2), channel_id=1, source_target_pairs={{0,16},{16,0},{1,17},{17,1},{2,18},{18,2},{3,19},{19,3},{4,20},{20... | collective-permute-start | bytes 688136 | tf_op jit(solution)/shard_map/cond/branch_0_fun/ppermute | solution.py:26
  142.6 11.1 %collective-permute-start.24 = (f32[28,16,128]{2,1,0:T(8,128)S(1)}, f32[28,16,128]{2,1,0:T(8,128)S(1)}, u32[]{:S(2)}, u32[]{:S(2)}) collective-permute-start(f32[28,16,128]{2,1,0:T(8,128)S(1)} %maximum_add_fusion.x_ref), channel_id=1, source_target_pairs={{0,0},{1,15},{2,14},{3,13},{4,12},{5,11},{6,10},{7,9},{8,8},{9,7},... | collective-permute-start | bytes 688136 | tf_op jit(solution)/shard_map/cond/branch_0_fun/ppermute | solution.py:293
  153.8 18.6 %collective-permute-start.25 = (f32[28,16,128]{2,1,0:T(8,128)S(1)}, f32[28,16,128]{2,1,0:T(8,128)S(1)}, u32[]{:S(2)}, u32[]{:S(2)}) collective-permute-start(f32[28,16,128]{2,1,0:T(8,128)S(1)} %collective-permute-done.24), channel_id=1, source_target_pairs={{0,0},{1,241},{2,226},{3,211},{4,196},{5,181},{6,166},{7,151},{8,1... | collective-permute-start | bytes 688136 | tf_op jit(solution)/shard_map/cond/branch_0_fun/ppermute | solution.py:293
  177.3 31.7 %copy-start.6 = (f32[4,16,1280]{2,1,0:T(8,128)}, f32[4,16,1280]{2,1,0:T(8,128)S(1)}, u32[]{:S(2)}) copy-start(f32[4,16,1280]{2,1,0:T(8,128)S(1)} %get-tuple-element.33) | copy-start | bytes 983044
  177.3 9.7 %collective-permute-start.29 = (f32[4,16,256]{2,1,0:T(8,128)S(1)}, f32[4,16,256]{2,1,0:T(8,128)S(1)}, u32[]{:S(2)}, u32[]{:S(2)}) collective-permute-start(f32[4,16,256]{2,1,0:T(8,128)S(1)} %get-tuple-element.38), channel_id=1, source_target_pairs={{0,31},{1,16},{2,17},{3,18},{4,19},{5,20},{6,21},{7,22},{8,23},{9,... | collective-permute-start | bytes 196616 | tf_op jit(solution)/shard_map/ppermute | solution.py:385
  187.1 6.2 %collective-permute-start.30 = (f32[4,16,256]{2,1,0:T(8,128)S(1)}, f32[4,16,256]{2,1,0:T(8,128)S(1)}, u32[]{:S(2)}, u32[]{:S(2)}) collective-permute-start(f32[4,16,256]{2,1,0:T(8,128)S(1)} %add.738), channel_id=1, source_target_pairs={{0,46},{1,47},{2,32},{3,33},{4,34},{5,35},{6,36},{7,37},{8,38},{9,... | collective-permute-start | bytes 196616 | tf_op jit(solution)/shard_map/ppermute | solution.py:385
  193.3 7.7 %collective-permute-start.31 = (f32[4,16,256]{2,1,0:T(8,128)S(1)}, f32[4,16,256]{2,1,0:T(8,128)S(1)}, u32[]{:S(2)}, u32[]{:S(2)}) collective-permute-start(f32[4,16,256]{2,1,0:T(8,128)S(1)} %add.739), channel_id=1, source_target_pairs={{0,76},{1,77},{2,78},{3,79},{4,64},{5,65},{6,66},{7,67},{8,68},{9,... | collective-permute-start | bytes 196616 | tf_op jit(solution)/shard_map/ppermute | solution.py:385
  201.0 8.0 %collective-permute-start.32 = (f32[4,16,256]{2,1,0:T(8,128)S(1)}, f32[4,16,256]{2,1,0:T(8,128)S(1)}, u32[]{:S(2)}, u32[]{:S(2)}) collective-permute-start(f32[4,16,256]{2,1,0:T(8,128)S(1)} %add.740), channel_id=1, source_target_pairs={{0,136},{1,137},{2,138},{3,139},{4,140},{5,141},{6,142},{7,143},{8... | collective-permute-start | bytes 196616 | tf_op jit(solution)/shard_map/ppermute | solution.py:385
  209.8 29.1 %copy-start.3 = (f32[1,256,256]{2,1,0:T(8,128)S(1)}, f32[1,256,256]{2,1,0:T(8,128)}, u32[]{:S(2)}) copy-start(f32[1,256,256]{2,1,0:T(8,128)} %param.10) | copy-start | bytes 786436
